TPU v7x, 32 devices: a whole 2x2x4 slice. The times are simulated.
32 devices in a mesh: expert: 16 (over z, y, x), dp: 2 (over core).
Axes of the slice: x: 2, y: 2, z: 4, core: 2. Of those that a mesh axis runs over, the one named last changes fastest.
Arguments:
- block_input: float32 [16384, 768], P(('expert', 'dp')), may hold values from -6 to 6
- cotangent: float32 [16384, 768], P(('expert', 'dp')), may hold values from -6 to 6
- segment_ids: int32 [32, 512], P(('expert', 'dp')), may hold values from 0 to 7, never falling along the last dimension, each value on 1 to 256 neighbouring positions
- routes: int32 [16384, 2], P(('expert', 'dp')), may hold values from 0 to 15, as said below
- slot_ids: int32 [16384, 2], P(('expert', 'dp')), may hold values from 0 to 127, as said below
- attention_in: bfloat16 [768, 2304], P('dp'), may hold values from -0.21875 to 0.21875
- attention_out: bfloat16 [768, 768], P('dp'), may hold values from -1.25 to 1.25
- router_weight: bfloat16 [768, 16], P('dp'), may hold values from -0.21875 to 0.21875
- first_gain: bfloat16 [768], P('dp'), may hold values from 0.099609375 to 1.8984375
- second_gain: bfloat16 [768], P('dp'), may hold values from 0.099609375 to 1.8984375
- bias_table: bfloat16 [32, 12], P('dp'), may hold values from -4 to 302
- expert_up: bfloat16 [16, 768, 3072], P('expert'), may hold values from -0.21875 to 0.21875
- expert_down: bfloat16 [16, 3072, 768], P('expert'), may hold values from -0.109375 to 0.109375
Outputs:
- block_output: float32 [16384, 768], P(('expert', 'dp'))
- input_grad: float32 [16384, 768], P(('expert', 'dp'))
- gradient_in: float32 [768, 2304], P('dp')
- gradient_out: float32 [768, 768], P('dp')
- gradient_router: float32 [768, 16], P('dp')
- gradient_first: float32 [768], P('dp')
- gradient_second: float32 [768], P('dp')
- gradient_bias: float32 [32, 12], P('dp')
- gradient_up: float32 [16, 768, 3072], P('expert', None, 'dp')
- gradient_down: float32 [16, 3072, 768], P('expert', 'dp')
Inputs may be any that keep to these rules, and one draw needn't show every extreme that they name: `routes`: the two experts of a row differ. Among the rows of one sequence no expert is named more than 128 times, and one expert, the same in every sequence, is named exactly 128 times. `slot_ids`: within one sequence, the slots of the rows naming one expert are distinct and are 0 up to the number of those rows - 1.
All inputs are finite; a program needn't handle non-finite values.
Results may differ from a plain program's by a relative error of at most 0.014.
Values may be sent and summed in bfloat16 or wider, within the bound.
A program may use at most 320 MiB of HBM per device.

v0:
```python
import functools
import math

import jax
import jax.numpy as jnp
import numpy as np
from jax import lax
from jax.experimental import pallas as pl
from jax.experimental.pallas import tpu as pltpu
from jax.sharding import PartitionSpec as P

EPS = 1e-06
F32 = jnp.float32
BF16 = jnp.bfloat16
BLOCK = 128
MASKED = -1e30


def reach_marks(buckets, reach_len):
    half_count = buckets // 2
    step_ids = np.arange(1, half_count)
    thresholds = np.floor(half_count * (reach_len / half_count) ** (step_ids / half_count))
    thresholds = np.maximum(thresholds, half_count + step_ids)
    return [int(mark) for mark in thresholds.astype(np.int32)]


def normal_cdf(argument):
    return 0.5 * (1.0 + jax.scipy.special.erf(argument * (1.0 / math.sqrt(2.0))))


def gelu_slope(argument):
    return normal_cdf(argument) + argument * (
        jnp.exp(-0.5 * argument * argument) * (1.0 / math.sqrt(2.0 * math.pi))
    )


def dot(left, right, left_dim=1, right_dim=0):
    return lax.dot_general(
        left, right, (((left_dim,), (right_dim,)), ((), ())), preferred_element_type=F32
    )


def bucket_hot(buckets, length, width):
    column = lax.broadcasted_iota(jnp.int32, (1, width), 1)
    distance = jnp.maximum(length // 2 + BLOCK - 1 - column, 0)
    bucket = jnp.minimum(distance, buckets // 2)
    for mark in reach_marks(buckets, length):
        bucket = bucket + jnp.where(distance >= mark, 1, 0)
    rows = lax.broadcasted_iota(jnp.int32, (buckets, width), 0)
    return jnp.where(rows == bucket, 1.0, 0.0)


def spans(length):
    reach = length // 2
    for block in range(length // BLOCK):
        low = max(0, block * BLOCK - reach)
        high = (block + 1) * BLOCK
        yield block, low, high, reach + BLOCK - (high - low)


def halves(pair):
    lane = lax.broadcasted_iota(jnp.int32, (1, pair.shape[1]), 1)
    first = lane < pair.shape[1] // 2
    zero = jnp.zeros_like(pair)
    return jnp.where(first, pair, zero), jnp.where(first, zero, pair)


def forward_kernel(
    x_ref, segment_ref, route_ref, in_ref, out_ref, router_ref, gain_ref, bias_ref,
    hidden_ref, normed_ref, triple_ref, context_ref, prob_ref, gate_ref,
    table_ref, mask_ref, one_ref,
):
    length, width = x_ref.shape
    heads, buckets = bias_ref.shape
    pair = 2 * (width // heads)
    pairs = heads // 2
    reach = length // 2
    span = reach + BLOCK
    scale = 1.0 / math.sqrt(width // heads)

    x = x_ref[...]
    rms = lax.rsqrt(jnp.mean(x * x, axis=1, keepdims=True) + EPS)
    one_ref[...] = (x * rms * gain_ref[0:1, :].astype(F32)).astype(BF16)

    chunk = 3 * pair

    def project(step, carry):
        columns = pl.ds(pl.multiple_of(step * chunk, BLOCK), chunk)
        triple_ref[:, columns] = dot(one_ref[...], in_ref[:, columns]).astype(BF16)
        return carry

    lax.fori_loop(0, 3 * width // chunk, project, 0)

    wide = span + BLOCK
    by_column = dot(bias_ref[...], bucket_hot(buckets, length, wide).astype(BF16))
    for head in range(heads):
        spread = jnp.broadcast_to(by_column[head : head + 1, :], (BLOCK, wide))
        rolled = pltpu.roll(spread, wide - BLOCK + 1, 1, stride=1, stride_axis=0)
        table_ref[head // 2, (head % 2) * BLOCK : (head % 2 + 1) * BLOCK, :] = rolled[:, :span]

    segment_row = segment_ref[...].astype(F32)
    segment_column = jnp.transpose(jnp.broadcast_to(segment_row, (BLOCK, length)))
    for block, low, high, skip in spans(length):
        rows = block * BLOCK + lax.broadcasted_iota(jnp.int32, (BLOCK, high - low), 0)
        columns = low + lax.broadcasted_iota(jnp.int32, (BLOCK, high - low), 1)
        own = segment_column[block * BLOCK : (block + 1) * BLOCK, 0:1]
        allowed = (rows >= columns) & (own == segment_row[:, low:high])
        mask_ref[block, :, skip:] = jnp.where(allowed, 0.0, MASKED)

    def attend(step, carry):
        base = pl.multiple_of(step * pair, pair)
        query_columns = pl.ds(base, pair)
        key_columns = pl.ds(pl.multiple_of(width + base, pair), pair)
        value_columns = pl.ds(pl.multiple_of(2 * width + base, pair), pair)
        for block, low, high, skip in spans(length):
            rows = slice(block * BLOCK, (block + 1) * BLOCK)
            query = triple_ref[rows, query_columns] * jnp.asarray(scale, BF16)
            stacked = jnp.concatenate(halves(query), axis=0)
            scores = dot(stacked, triple_ref[low:high, key_columns], 1, 1)
            mask = mask_ref[block, :, skip:]
            scores = scores + table_ref[step, :, skip:] + jnp.concatenate([mask, mask], axis=0)
            top = jnp.max(scores, axis=1, keepdims=True)
            weight = jnp.exp(scores - top)
            prob = weight * (1.0 / jnp.sum(weight, axis=1, keepdims=True))
            half = prob.astype(BF16)
            prob_ref[step, block, :, skip:] = half
            first, second = halves(triple_ref[low:high, value_columns])
            context = dot(half[:BLOCK], first) + dot(half[BLOCK:], second)
            context_ref[rows, query_columns] = context.astype(BF16)
        return carry

    lax.fori_loop(0, pairs, attend, 0)

    hidden = x_ref[...] + dot(context_ref[...], out_ref[...])
    hidden_ref[...] = hidden
    rms = lax.rsqrt(jnp.mean(hidden * hidden, axis=1, keepdims=True) + EPS)
    normed = (hidden * rms * gain_ref[1:2, :].astype(F32)).astype(BF16)
    normed_ref[...] = normed
    logits = dot(router_ref[...], normed, 1, 1)
    expert_ids = lax.broadcasted_iota(jnp.int32, logits.shape, 0)
    first = jnp.sum(jnp.where(expert_ids == route_ref[0:1, :], logits, 0.0), axis=0, keepdims=True)
    second = jnp.sum(jnp.where(expert_ids == route_ref[1:2, :], logits, 0.0), axis=0, keepdims=True)
    gate_ref[0:1, :] = 1.0 / (1.0 + jnp.exp(second - first))
    gate_ref[1:2, :] = 1.0 / (1.0 + jnp.exp(first - second))


def backward_kernel(
    x_ref, hidden_grad_ref, triple_ref, context_ref, prob_ref, in_ref, out_ref, gain_ref,
    input_grad_ref, in_grad_ref, out_grad_ref, gain_grad_ref, bias_grad_ref,
    context_grad_ref, triple_grad_ref, turned_ref, key_ref, value_ref, diagonal_ref, sums_ref,
):
    length, width = x_ref.shape
    buckets, heads = bias_grad_ref.shape
    pair = 2 * (width // heads)
    pairs = heads // 2
    reach = length // 2
    span = reach + BLOCK
    scale = 1.0 / math.sqrt(width // heads)

    residual = hidden_grad_ref[...].astype(BF16)
    context_grad_ref[...] = dot(residual, out_ref[...], 1, 1).astype(BF16)
    out_grad_ref[...] = dot(jnp.transpose(context_ref[...]), residual)
    diagonal_ref[...] = jnp.zeros_like(diagonal_ref)

    def attend(step, carry):
        base = pl.multiple_of(step * pair, pair)
        query_columns = pl.ds(base, pair)
        key_columns = pl.ds(pl.multiple_of(width + base, pair), pair)
        value_columns = pl.ds(pl.multiple_of(2 * width + base, pair), pair)
        key_ref[...] = jnp.zeros_like(key_ref)
        value_ref[...] = jnp.zeros_like(value_ref)
        for block, low, high, skip in spans(length):
            rows = slice(block * BLOCK, (block + 1) * BLOCK)
            query = triple_ref[rows, query_columns] * jnp.asarray(scale, BF16)
            query = jnp.concatenate(halves(query), axis=0)
            grad = jnp.concatenate(halves(context_grad_ref[rows, query_columns]), axis=0)
            half = prob_ref[step, block, :, skip:]
            prob = half.astype(F32)
            prob_grad = dot(grad, triple_ref[low:high, value_columns], 1, 1)
            row_dot = jnp.sum(prob * prob_grad, axis=1, keepdims=True)
            score_grad = prob * (prob_grad - row_dot)
            diagonal_ref[step, :, skip:] += score_grad
            score_half = score_grad.astype(BF16)
            first, second = halves(triple_ref[low:high, key_columns])
            query_grad = dot(score_half[:BLOCK], first) + dot(score_half[BLOCK:], second)
            triple_grad_ref[rows, query_columns] = (query_grad * scale).astype(BF16)
            key_ref[low:high, :] += dot(score_half, query, 0, 0)
            value_ref[low:high, :] += dot(half, grad, 0, 0)
        triple_grad_ref[:, key_columns] = key_ref[...].astype(BF16)
        triple_grad_ref[:, value_columns] = value_ref[...].astype(BF16)
        return carry

    lax.fori_loop(0, pairs, attend, 0)

    x = x_ref[...]
    rms = lax.rsqrt(jnp.mean(x * x, axis=1, keepdims=True) + EPS)
    gain = gain_ref[0:1, :].astype(F32)
    turned_ref[...] = jnp.transpose((x * rms * gain).astype(BF16))
    chunk = 3 * pair

    def weigh(step, carry):
        columns = pl.ds(pl.multiple_of(step * chunk, BLOCK), chunk)
        in_grad_ref[:, columns] = dot(turned_ref[...], triple_grad_ref[:, columns])
        return carry

    lax.fori_loop(0, 3 * width // chunk, weigh, 0)

    gain_grad_ref[...] = jnp.zeros_like(gain_grad_ref)

    def finish(step, carry):
        rows = pl.ds(pl.multiple_of(step * BLOCK, BLOCK), BLOCK)
        normed_grad = dot(triple_grad_ref[rows, :], in_ref[...], 1, 1)
        part = x_ref[rows, :]
        scaling = lax.rsqrt(jnp.mean(part * part, axis=1, keepdims=True) + EPS)
        gain_grad_ref[...] += jnp.sum(normed_grad * (part * scaling), axis=0, keepdims=True)
        scaled = normed_grad * gain
        inner = jnp.mean(scaled * part, axis=1, keepdims=True)
        input_grad_ref[rows, :] = hidden_grad_ref[rows, :] + (
            scaling * scaled - part * (scaling * scaling * scaling) * inner
        )
        return carry

    lax.fori_loop(0, length // BLOCK, finish, 0)

    wide = span + BLOCK
    row_ids = lax.broadcasted_iota(jnp.int32, (BLOCK, wide), 0)
    for head in range(heads):
        sheet = diagonal_ref[head // 2, (head % 2) * BLOCK : (head % 2 + 1) * BLOCK, :]
        sheet = jnp.concatenate([sheet, jnp.zeros((BLOCK, BLOCK), F32)], axis=1)
        sheet = pltpu.roll(sheet, BLOCK - 1, 1)
        step = 1
        while step < BLOCK:
            sheet = jnp.where((row_ids & step) != 0, pltpu.roll(sheet, wide - step, 1), sheet)
            step *= 2
        sums_ref[head : head + 1, :] = jnp.sum(sheet, axis=0, keepdims=True)
    hot = bucket_hot(buckets, length, wide).astype(BF16)
    rest = sums_ref[...]
    total = jnp.zeros((buckets, heads), F32)
    for _ in range(3):
        piece = rest.astype(BF16)
        total = total + dot(hot, piece, 1, 1)
        rest = rest - piece.astype(F32)
    bias_grad_ref[...] = total


def whole(count):
    return [pl.BlockSpec(memory_space=pltpu.VMEM)] * count


def params(**extra):
    return pltpu.CompilerParams(vmem_limit_bytes=60 * 2**20, **extra)


def forward(x, segments, route_rows, full_in, full_out, router_rows, gains, bias_rows):
    length, width = x.shape
    heads = bias_rows.shape[0]
    blocks, span = length // BLOCK, length // 2 + BLOCK
    shape = jax.ShapeDtypeStruct
    return pl.pallas_call(
        forward_kernel,
        out_shape=(
            shape((length, width), F32),
            shape((length, width), BF16),
            shape((length, 3 * width), BF16),
            shape((length, width), BF16),
            shape((heads // 2, blocks, 2 * BLOCK, span), BF16),
            shape((2, length), F32),
        ),
        in_specs=whole(8),
        out_specs=tuple(whole(6)),
        scratch_shapes=[
            pltpu.VMEM((heads // 2, 2 * BLOCK, span), F32),
            pltpu.VMEM((blocks, BLOCK, span), F32),
            pltpu.VMEM((length, width), BF16),
        ],
        compiler_params=params(),
        cost_estimate=pl.CostEstimate(
            flops=12 * 10**9, bytes_accessed=2 * 10**7, transcendentals=2 * 10**6
        ),
        name="attention_forward",
    )(x, segments, route_rows, full_in, full_out, router_rows, gains, bias_rows)


def backward(x, hidden_grad, triple, context, probs, full_in, full_out, gains, buckets):
    length, width = x.shape
    pairs, blocks, _, span = probs.shape
    shape = jax.ShapeDtypeStruct
    return pl.pallas_call(
        backward_kernel,
        out_shape=(
            shape((length, width), F32),
            shape((width, 3 * width), F32),
            shape((width, width), F32),
            shape((1, width), F32),
            shape((buckets, 2 * pairs), F32),
        ),
        in_specs=whole(8),
        out_specs=tuple(whole(5)),
        scratch_shapes=[
            pltpu.VMEM((length, width), BF16),
            pltpu.VMEM((length, 3 * width), BF16),
            pltpu.VMEM((width, length), BF16),
            pltpu.VMEM((length, 2 * (width // (2 * pairs))), F32),
            pltpu.VMEM((length, 2 * (width // (2 * pairs))), F32),
            pltpu.VMEM((pairs, 2 * BLOCK, span), F32),
            pltpu.VMEM((2 * pairs, span + BLOCK), F32),
        ],
        compiler_params=params(),
        cost_estimate=pl.CostEstimate(
            flops=25 * 10**9, bytes_accessed=3 * 10**7, transcendentals=2 * 10**6
        ),
        name="attention_backward",
    )(x, hidden_grad, triple, context, probs, full_in, full_out, gains)


def shards(
    block_input,
    cotangent,
    segment_ids,
    routes,
    slot_ids,
    attention_in,
    attention_out,
    router_weight,
    first_gain,
    second_gain,
    bias_table,
    expert_up,
    expert_down,
):
    length, width = block_input.shape
    owners = lax.axis_size("expert")
    capacity = 4 * length // owners
    experts = router_weight.shape[1]
    slots = experts * capacity

    place = routes * capacity + slot_ids
    slot_range = jnp.arange(slots, dtype=jnp.int32)[None, :]
    match_first = place[:, 0:1] == slot_range
    match_second = place[:, 1:2] == slot_range
    hot_first = match_first.astype(BF16)
    hot_second = match_second.astype(BF16)
    hot_both = (match_first | match_second).astype(BF16)

    def exchange(rows):
        return lax.all_to_all(
            rows.reshape(owners, -1, rows.shape[-1]), "expert", split_axis=0, concat_axis=0, tiled=True
        )

    cot_rows = exchange(dot(hot_both, cotangent.astype(BF16), 0, 0).astype(BF16))
    full_in, full_out, full_router, gains, bias_small = (
        lax.all_gather(attention_in, "dp", axis=0, tiled=True),
        lax.all_gather(attention_out, "dp", axis=0, tiled=True),
        lax.all_gather(router_weight, "dp", axis=0, tiled=True),
        lax.all_gather(jnp.stack([first_gain, second_gain]), "dp", axis=1, tiled=True),
        lax.all_gather(bias_table, "dp", axis=0, tiled=True),
    )
    buckets = bias_small.shape[0]
    hidden_state, normed_two, triple, context, probs, gates = forward(
        block_input, segment_ids, routes.T, full_in, full_out, full_router.T, gains, bias_small.T
    )
    gate_first, gate_second = gates[0], gates[1]
    rms_two = lax.rsqrt(jnp.mean(hidden_state * hidden_state, axis=1, keepdims=True) + EPS)
    normal_two = hidden_state * rms_two
    expert_ids = jnp.arange(experts, dtype=jnp.int32)
    pick_first = (routes[:, 0:1] == expert_ids[None, :]).astype(F32)
    pick_second = (routes[:, 1:2] == expert_ids[None, :]).astype(F32)
    slot_gates = jnp.sum(
        jnp.where(match_first, gate_first[:, None], 0.0)
        + jnp.where(match_second, gate_second[:, None], 0.0),
        axis=0,
    )
    slot_gates = exchange(slot_gates.reshape(owners, 1, -1))
    up_matrix = expert_up[0]
    down_matrix = expert_down[0]
    flat_rows = exchange(dot(hot_both, normed_two, 0, 0).astype(BF16)).reshape(-1, width)
    expert_pre = dot(flat_rows, up_matrix)
    activation = (expert_pre * normal_cdf(expert_pre)).astype(BF16)
    produced = dot(activation, down_matrix).astype(BF16)
    returned = exchange(produced).reshape(slots, width)
    picked_first = dot(hot_first, returned)
    picked_second = dot(hot_second, returned)
    block_output = hidden_state + (
        gate_first[:, None] * picked_first + gate_second[:, None] * picked_second
    )
    gate_grad_first = jnp.sum(cotangent * picked_first, axis=1)
    gate_grad_second = jnp.sum(cotangent * picked_second, axis=1)
    logit_delta = gate_first * gate_second * (gate_grad_first - gate_grad_second)
    logit_grad = ((pick_first - pick_second) * logit_delta[:, None]).astype(BF16)
    flat_grad = (slot_gates.reshape(-1)[:, None] * cot_rows.reshape(-1, width).astype(F32)).astype(
        BF16
    )
    act_grad = dot(flat_grad, down_matrix, 1, 1)
    pre_grad = (act_grad * gelu_slope(expert_pre)).astype(BF16)
    grad_down = dot(activation, flat_grad, 0, 0)
    grad_up = dot(flat_rows, pre_grad, 0, 0)
    back_rows = dot(pre_grad, up_matrix, 1, 1).astype(BF16)
    home_rows = exchange(back_rows).reshape(slots, width)
    normed_grad = dot(hot_both, home_rows) + dot(logit_grad, full_router, 1, 1)
    router_grad = dot(normed_two, logit_grad, 0, 0)
    second_grad = jnp.sum(normed_grad * normal_two, axis=0)
    scaled_two = normed_grad * gains[1:2].astype(F32)
    hidden_grad = cotangent + (
        rms_two * scaled_two
        - hidden_state
        * (rms_two * rms_two * rms_two)
        * jnp.mean(scaled_two * hidden_state, axis=1, keepdims=True)
    )
    input_grad, triple_weight, proj_grad, first_grad, bias_grad = backward(
        block_input, hidden_grad, triple, context, probs, full_in, full_out, gains, buckets
    )
    member = lax.axis_index("dp")
    pair_size = lax.axis_size("dp")
    big = jnp.concatenate([triple_weight, proj_grad], axis=1)
    big = lax.psum(lax.psum_scatter(big, "dp", scatter_dimension=0, tiled=True), "expert")
    small = lax.psum((router_grad, first_grad[0], second_grad, bias_grad), ("expert", "dp"))
    small = [
        lax.dynamic_slice_in_dim(
            gradient, member * (gradient.shape[0] // pair_size), gradient.shape[0] // pair_size, 0
        )
        for gradient in small
    ]
    up_share, down_share = (
        lax.psum_scatter(
            grad_up[None].astype(BF16), "dp", scatter_dimension=2, tiled=True
        ).astype(F32),
        lax.psum_scatter(
            grad_down[None].astype(BF16), "dp", scatter_dimension=1, tiled=True
        ).astype(F32),
    )
    return (
        block_output,
        input_grad,
        big[:, : 3 * width],
        big[:, 3 * width :],
        small[0],
        small[1],
        small[2],
        small[3],
        up_share,
        down_share,
    )


def solution(mesh):
    rows = P(("expert", "dp"), None)
    return jax.shard_map(
        shards,
        mesh=mesh,
        in_specs=(
            rows,
            rows,
            rows,
            rows,
            rows,
            P("dp", None),
            P("dp", None),
            P("dp", None),
            P("dp"),
            P("dp"),
            P("dp", None),
            P("expert", None, None),
            P("expert", None, None),
        ),
        out_specs=(
            rows,
            rows,
            P("dp", None),
            P("dp", None),
            P("dp", None),
            P("dp"),
            P("dp"),
            P("dp", None),
            P("expert", None, "dp"),
            P("expert", "dp", None),
        ),
        check_vma=False,
    )
```

profile of v0, /device:TPU:12, one launch (start us, length us, event | category | flops | bytes accessed | tf_op | source)
XLA Modules:
  0.0 728.0 jit_solution(9083656691927942198)
XLA Ops:
  20.2 15.5 %all-gather.3.cloned.1.call-done.in_ref = bf16[768,2304]{1,0:T(8,128)(2,1)} async-done(((bf16[384,2304]{1,0:T(8,128)(2,1)}), bf16[768,2304]{1,0:T(8,128)(2,1)}) %all-gather.3.cloned.1.call-update) | async-done | bytes 3538960 | tf_op jit(solution)/shard_map/all_gather | solution.py:352
  35.6 21.5 %attention_forward.1 = (f32[512,768]{1,0:T(8,128)}, bf16[512,768]{1,0:T(8,128)(2,1)}, bf16[512,2304]{1,0:T(8,128)(2,1)}, bf16[512,768]{1,0:T(8,128)(2,1)}, bf16[...) custom-call(f32[512,768]{1,0:T(8,128)} %x_ref.3, s32[1,512]{1,0:T(1,128)} %segment_ref.1, s32[2,512]{1,0:T(2,128)} %bitcast.66, ...), custom_call_target="tpu_custom_call" | custom-call | flops 12000000000 | bytes 20000000 | tf_op jit(solution)/shard_map/attention_forward/pallas_call | solution.py:259
  59.9 7.0 all-to-all-start.2
  71.9 5.9 all-to-all-start.3
  77.8 4.9 convolution_convert_fusion.3
  82.6 65.1 %all-to-all-done.3 = bf16[16,128,768]{2,1,0:T(8,128)(2,1)S(1)} async-done(((bf16[16,128,768]{2,1,0:T(8,128)(2,1)}), bf16[16,128,768]{2,1,0:T(8,128)(2,1)S(1)}, u32[]{:S(2)}, u32[]{:S(2)}) %all-to-all-start.3) | async-done | bytes 3145760 | tf_op jit(solution)/shard_map/all_to_all | solution.py:346
  147.7 6.0 all-to-all-start
  156.0 67.5 %all-to-all-done = bf16[16,128,768]{2,1,0:T(8,128)(2,1)} async-done(((bf16[16,128,768]{2,1,0:T(8,128)(2,1)}), bf16[16,128,768]{2,1,0:T(8,128)(2,1)}, u32[]{:S(2)}, u32[]{:S(2)}) %all-to-all-start) | async-done | bytes 3145760 | tf_op jit(solution)/shard_map/all_to_all | solution.py:346
  223.6 18.8 %multiply_convert_fusion = (bf16[2048,3072]{1,0:T(8,128)(2,1)}, f32[2048,3072]{1,0:T(8,128)}) fusion(bf16[2048,768]{1,0:T(8,128)(2,1)} %bitcast.7, bf16[1,768,3072]{2,1,0:T(8,128)(2,1)} %param.24), kind=kOutput, calls=%fused_computation.7 | convolution fusion | flops 9695133696 | bytes 45613056 | tf_op jit(solution)/shard_map/dot_general | solution.py:38
  242.4 21.0 %fusion.5 = bf16[2048,3072]{1,0:T(8,128)(2,1)S(1)} fusion(f32[2048,3072]{1,0:T(8,128)} %get-tuple-element.51, bf16[2048,768]{1,0:T(8,128)(2,1)S(1)} %bitcast.61, bf16[1,3072,768]{2,1,0:T(8,128)(2,1)} %param.25), kind=kOutput, calls=%fused_computation.6 | convolution fusion | flops 9726590976 | bytes 45613056 | tf_op jit(solution)/shard_map/dot_general | solution.py:38
  263.4 11.3 %fusion.19 = bf16[2048,768]{1,0:T(8,128)(2,1)} fusion(bf16[2048,3072]{1,0:T(8,128)(2,1)S(1)} %fusion.5, bf16[1,768,3072]{2,1,0:T(8,128)(2,1)S(1)} %bitcast.89), kind=kOutput, calls=%fused_computation.30 | convolution fusion | flops 9665249280 | bytes 20447232 | tf_op jit(solution)/shard_map/dot_general | solution.py:38
  274.7 5.1 all-to-all-start.4
  279.9 15.4 %fusion.22 = bf16[2048,768]{1,0:T(8,128)(2,1)} fusion(bf16[2048,3072]{1,0:T(8,128)(2,1)} %get-tuple-element.50, bf16[1,3072,768]{2,1,0:T(8,128)(2,1)} %param.25), kind=kOutput, calls=%fused_computation.31 | convolution fusion | flops 9665249280 | bytes 20447232 | tf_op jit(solution)/shard_map/dot_general | solution.py:38
  295.3 54.4 %all-to-all-done.4 = bf16[16,128,768]{2,1,0:T(8,128)(2,1)} async-done(((bf16[16,128,768]{2,1,0:T(8,128)(2,1)}), bf16[16,128,768]{2,1,0:T(8,128)(2,1)}, u32[]{:S(2)}, u32[]{:S(2)}) %all-to-all-start.4) | async-done | bytes 3145760 | tf_op jit(solution)/shard_map/all_to_all | solution.py:346
  349.7 4.8 all-to-all-start.1
  354.6 5.3 fusion.25
  359.9 64.6 %all-to-all-done.1 = bf16[16,128,768]{2,1,0:T(8,128)(2,1)} async-done(((bf16[16,128,768]{2,1,0:T(8,128)(2,1)}), bf16[16,128,768]{2,1,0:T(8,128)(2,1)}, u32[]{:S(2)}, u32[]{:S(2)}) %all-to-all-start.1) | async-done | bytes 3145760 | tf_op jit(solution)/shard_map/all_to_all | solution.py:346
  428.6 5.5 multiply_reduce_fusion.2
  436.5 35.4 %attention_backward.1 = (f32[512,768]{1,0:T(8,128)}, f32[768,2304]{1,0:T(8,128)}, f32[768,768]{1,0:T(8,128)}, f32[1,768]{1,0:T(1,128)}, f32[32,12]{1,0:T(8,128)}) custom-call(f32[512,768]{1,0:T(8,128)} %x_ref.3, f32[512,768]{1,0:T(8,128)} %subtract_add_fusion.hidden_grad_ref, bf16[512,2304]{1,0:T(8,128)(2,1)} %get-tuple-element.24.triple_ref, ...), custom_call_target="tpu_custom_call" | custom-call | flops 24999999488 | bytes 30000000 | tf_op jit(solution)/shard_map/attention_backward/pallas_call | solution.py:288
  471.9 8.7 %pad_maximum_fusion = f32[768,3072]{1,0:T(8,128)} fusion(f32[768,768]{1,0:T(8,128)} %get-tuple-element.29, f32[768,2304]{1,0:T(8,128)} %get-tuple-element.28), kind=kLoop, calls=%fused_computation.9 | loop fusion | flops 2359296 | bytes 18874368 | tf_op jit(solution)/shard_map/concatenate | solution.py:414
  481.2 14.8 %fusion.15 = bf16[1,3072,768]{2,1,0:T(8,128)(2,1)} fusion(bf16[2048,3072]{1,0:T(8,128)(2,1)} %get-tuple-element.50, bf16[2048,768]{1,0:T(8,128)(2,1)S(1)} %fusion.6), kind=kOutput, calls=%fused_computation.23 | convolution fusion | flops 9666035712 | bytes 20447232 | tf_op jit(solution)/shard_map/dot_general | solution.py:38
  496.1 15.5 %fusion.14 = bf16[1,768,3072]{2,1,0:T(8,128)(2,1)} fusion(bf16[2048,768]{1,0:T(8,128)(2,1)} %bitcast.7, bf16[2048,3072]{1,0:T(8,128)(2,1)} %copy-done.11), kind=kOutput, calls=%fused_computation.22 | convolution fusion | flops 9666035712 | bytes 20447232 | tf_op jit(solution)/shard_map/dot_general | solution.py:38
  513.2 41.4 %all-reduce = (f32[768,16]{0,1:T(8,128)S(1)}, f32[768]{0:T(1024)S(1)}, f32[768]{0:T(1024)S(1)}, f32[32,12]{1,0:T(8,128)S(1)}) all-reduce(f32[768,16]{0,1:T(8,128)S(1)} %fusion.38, f32[768]{0:T(1024)S(1)} %reduce.1, f32[768]{0:T(1024)S(1)} %get-tuple-element.32, ...), channel_id=1, replica_groups=mesh['expert'=16,'dp'=2] {'expert','dp'}, use_global_device_ids=true, to_apply=%region_7.8 | all-reduce | flops 14208 | bytes 113664 | tf_op jit(solution)/shard_map/psum | solution.py:416
  565.9 148.4 %all-reduce.3.cloned.1.call-done = f32[384,3072]{1,0:T(8,128)} async-done(((f32[384,3072]{1,0:T(8,128)}), f32[384,3072]{1,0:T(8,128)}) %all-reduce.3.cloned.1.call-update) | async-done | bytes 4718608 | tf_op jit(solution)/shard_map/psum | solution.py:415
  (78 shorter events, 49.4 us)
Async XLA Ops:
  7.2 13.0 %all-gather.5.cloned.1.call-start = ((), (), s32[]{:S(2)}) async-start(), calls=%async_computation.9 | async-start | bytes 1769472 | tf_op jit(solution)/shard_map/all_gather | solution.py:353
  7.9 27.7 %all-gather.3.cloned.1.call-start = ((), (), s32[]{:S(2)}) async-start(), calls=%async_computation.8 | async-start | bytes 5308416 | tf_op jit(solution)/shard_map/all_gather | solution.py:352
  35.6 31.3 %copy-start.2 = (f32[512,768]{1,0:T(8,128)S(1)}, f32[512,768]{1,0:T(8,128)}, u32[]{:S(2)}) copy-start(f32[512,768]{1,0:T(8,128)} %param.14) | copy-start | bytes 4718596
  59.9 11.9 %all-to-all-start.2 = ((f32[16,1,128]{2,1,0:T(1,128)}), f32[16,1,128]{2,1,0:T(1,128)S(1)}, u32[]{:S(2)}, u32[]{:S(2)}) async-start(f32[16,1,128]{2,1,0:T(1,128)} %bitcast.13), calls=%async_computation.2 | async-start | bytes 16384 | tf_op jit(solution)/shard_map/all_to_all | solution.py:346
  71.9 75.9 %all-to-all-start.3 = ((bf16[16,128,768]{2,1,0:T(8,128)(2,1)}), bf16[16,128,768]{2,1,0:T(8,128)(2,1)S(1)}, u32[]{:S(2)}, u32[]{:S(2)}) async-start(bf16[16,128,768]{2,1,0:T(8,128)(2,1)} %bitcast.59), calls=%async_computation.3 | async-start | bytes 6291456 | tf_op jit(solution)/shard_map/all_to_all | solution.py:346
  147.7 75.8 %all-to-all-start = ((bf16[16,128,768]{2,1,0:T(8,128)(2,1)}), bf16[16,128,768]{2,1,0:T(8,128)(2,1)}, u32[]{:S(2)}, u32[]{:S(2)}) async-start(bf16[16,128,768]{2,1,0:T(8,128)(2,1)} %bitcast.60), calls=%async_computation | async-start | bytes 6291456 | tf_op jit(solution)/shard_map/all_to_all | solution.py:346
  223.5 18.8 %copy-start.1 = (bf16[16,128,768]{2,1,0:T(8,128)(2,1)S(1)}, bf16[16,128,768]{2,1,0:T(8,128)(2,1)}, u32[]{:S(2)}) copy-start(bf16[16,128,768]{2,1,0:T(8,128)(2,1)} %multiply_convert_fusion.1) | copy-start | bytes 9437188
  223.5 39.8 %slice-start = ((s8[4718592]{0:T(1024)(128)(4,1)}), s8[4194304]{0:T(1024)(128)(4,1)S(1)}, s32[]{:S(2)}) async-start(s8[4718592]{0:T(1024)(128)(4,1)} %bitcast.88), calls=%async_computation.14 | async-start | bytes 8388608
  242.4 21.0 %slice-start.1 = ((s8[4718592]{0:T(1024)(128)(4,1)}), s8[524288]{0:T(1024)(128)(4,1)S(1)}, s32[]{:S(2)}) async-start(s8[4718592]{0:T(1024)(128)(4,1)} %bitcast.88), calls=%async_computation.15 | async-start | bytes 1048576
  263.4 11.3 %copy-start.11 = (bf16[2048,3072]{1,0:T(8,128)(2,1)}, bf16[2048,3072]{1,0:T(8,128)(2,1)S(1)}, u32[]{:S(2)}) copy-start(bf16[2048,3072]{1,0:T(8,128)(2,1)S(1)} %fusion.5) | copy-start | bytes 37748740
  274.7 74.9 %all-to-all-start.4 = ((bf16[16,128,768]{2,1,0:T(8,128)(2,1)}), bf16[16,128,768]{2,1,0:T(8,128)(2,1)}, u32[]{:S(2)}, u32[]{:S(2)}) async-start(bf16[16,128,768]{2,1,0:T(8,128)(2,1)} %bitcast.62), calls=%async_computation.4 | async-start | bytes 6291456 | tf_op jit(solution)/shard_map/all_to_all | solution.py:346
  295.3 59.3 %copy-start.8 = (bf16[2,768]{1,0:T(2,128)(2,1)S(1)}, bf16[2,768]{1,0:T(2,128)(2,1)}, u32[]{:S(2)}) copy-start(bf16[2,768]{1,0:T(2,128)(2,1)} %all_gather.18.gain_ref) | copy-start | bytes 9220
  295.3 59.3 %copy-start.6 = (s32[512,2]{0,1:T(2,128)S(1)}, s32[512,2]{0,1:T(2,128)}, u32[]{:S(2)}) copy-start(s32[512,2]{0,1:T(2,128)} %param.16) | copy-start | bytes 12292
  349.7 74.9 %all-to-all-start.1 = ((bf16[16,128,768]{2,1,0:T(8,128)(2,1)}), bf16[16,128,768]{2,1,0:T(8,128)(2,1)}, u32[]{:S(2)}, u32[]{:S(2)}) async-start(bf16[16,128,768]{2,1,0:T(8,128)(2,1)} %bitcast.58), calls=%async_computation.1 | async-start | bytes 6291456 | tf_op jit(solution)/shard_map/all_to_all | solution.py:346
  354.5 157.1 %reduce-scatter.4.cloned.1.call-start = ((), (), s32[]{:S(2)}) async-start(), calls=%async_computation.10 | async-start | bytes 14155776 | tf_op jit(solution)/shard_map/reduce_scatter | solution.py:415
  424.5 4.0 copy-start
  424.5 4.0 copy-start.3
  428.5 5.6 copy-start.4
  428.6 5.6 copy-start.5
  480.6 76.6 %reduce-scatter.8.cloned.1.call-start = ((), (), s32[]{:S(2)}) async-start(), calls=%async_computation.13 | async-start | bytes 7077888 | tf_op jit(solution)/shard_map/reduce_scatter | solution.py:427
  496.0 65.4 %reduce-scatter.6.cloned.1.call-start = ((), (), s32[]{:S(2)}) async-start(), calls=%async_computation.12 | async-start | bytes 7077888 | tf_op jit(solution)/shard_map/reduce_scatter | solution.py:424
  511.5 1.2 copy-start.10
  511.5 1.7 copy-start.7
  511.6 202.7 %all-reduce.3.cloned.1.call-start = ((), (), s32[]{:S(2)}) async-start(), calls=%async_computation.11 | async-start | bytes 9437184 | tf_op jit(solution)/shard_map/psum | solution.py:415
  (1 other events, 0.7 us)
Sparse Core Ops, SparseCore 0:
  9.5 10.5 all-gather.4
  21.7 13.8 all-gather.2
  480.7 16.3 reduce-scatter.3
  499.8 13.8 reduce-scatter.7
  516.4 13.6 reduce-scatter.5
  535.7 178.5 all-reduce.2
where the time goes:
time: 739 us; the launch traced here: 728 us
  waiting for transfers between devices  420 us (57%)
  matrix products  121 us (16%)
  Pallas kernels  56.8 us (8%)
  blocking collectives  48.4 us (7%)
  starting transfers between devices  29.1 us (4%)
  other arithmetic  24.6 us (3%)
  between operations  14.8 us (2%)
  local copies, waits for them, and re-layouts  12.4 us (2%)
    all_to_all x5, waiting for transfers between devices, exchange(): lax.all_to_all(rows.reshape(owners, -1, rows.shape[-1]), 'expert', split_...  253 us
    psum x1, waiting for transfers between devices, shards(): lax.psum(lax.psum_scatter(big, 'dp', scatter_dimension=0, tiled=True), 'e...  148 us
    dot_general x13, matrix products, dot(): lax.dot_general(left, right, (((left_dim,), (right_dim,)), ((), ())), pre...  121 us
    psum x1, blocking collectives, shards(): lax.psum((router_grad, first_grad[0], second_grad, bias_grad), ('expert',...  41.4 us
    pallas_call x1, Pallas kernels, backward(): pl.pallas_call(backward_kernel, out_shape=(shape((length, width), F32), s...  35.4 us
    all_to_all x5, starting transfers between devices, exchange(): lax.all_to_all(rows.reshape(owners, -1, rows.shape[-1]), 'expert', split_...  28.8 us
    pallas_call x1, Pallas kernels, forward(): pl.pallas_call(forward_kernel, out_shape=(shape((length, width), F32), sh...  21.5 us
    all_gather x1, waiting for transfers between devices, shards(): lax.all_gather(attention_in, 'dp', axis=0, tiled=True)  15.5 us
  transfers between devices with their start and end apart: 11, of which 8 were waited for; matrix products, arithmetic and copies ran while one was open for 11% of the time, Pallas kernels for 0%

commit v1 on v0

v1 whole, which is shorter than its diff:
```python
import functools
import math

import jax
import jax.numpy as jnp
import numpy as np
from jax import lax
from jax.experimental import pallas as pl
from jax.experimental.pallas import tpu as pltpu
from jax.sharding import PartitionSpec as P

EPS = 1e-06
F32 = jnp.float32
BF16 = jnp.bfloat16
BLOCK = 128
MASKED = -1e30


def reach_marks(buckets, reach_len):
    half_count = buckets // 2
    step_ids = np.arange(1, half_count)
    thresholds = np.floor(half_count * (reach_len / half_count) ** (step_ids / half_count))
    thresholds = np.maximum(thresholds, half_count + step_ids)
    return [int(mark) for mark in thresholds.astype(np.int32)]


def normal_cdf(argument):
    return 0.5 * (1.0 + jax.scipy.special.erf(argument * (1.0 / math.sqrt(2.0))))


def gelu_slope(argument):
    return normal_cdf(argument) + argument * (
        jnp.exp(-0.5 * argument * argument) * (1.0 / math.sqrt(2.0 * math.pi))
    )


def dot(left, right, left_dim=1, right_dim=0):
    return lax.dot_general(
        left, right, (((left_dim,), (right_dim,)), ((), ())), preferred_element_type=F32
    )


def bucket_hot(buckets, length, width):
    column = lax.broadcasted_iota(jnp.int32, (1, width), 1)
    distance = jnp.maximum(length // 2 + BLOCK - 1 - column, 0)
    bucket = jnp.minimum(distance, buckets // 2)
    for mark in reach_marks(buckets, length):
        bucket = bucket + jnp.where(distance >= mark, 1, 0)
    rows = lax.broadcasted_iota(jnp.int32, (buckets, width), 0)
    return jnp.where(rows == bucket, 1.0, 0.0)


def spans(length):
    reach = length // 2
    for block in range(length // BLOCK):
        low = max(0, block * BLOCK - reach)
        high = (block + 1) * BLOCK
        yield block, low, high, reach + BLOCK - (high - low)


def halves(pair):
    lane = lax.broadcasted_iota(jnp.int32, (1, pair.shape[1]), 1)
    first = lane < pair.shape[1] // 2
    zero = jnp.zeros_like(pair)
    return jnp.where(first, pair, zero), jnp.where(first, zero, pair)


def hot_rows(place_ref, first, count):
    ids = first + lax.broadcasted_iota(jnp.int32, (count, place_ref.shape[1]), 0)
    return ids == place_ref[0:1, :], ids == place_ref[1:2, :]


def bf16_of(flags):
    return jnp.where(flags, 1.0, 0.0).astype(BF16)


def pieces_of(row):
    parts = []
    for _ in range(3):
        piece = row.astype(BF16).astype(F32)
        parts.append(piece)
        row = row - piece
    parts.append(jnp.zeros((5, row.shape[1]), F32))
    return jnp.concatenate(parts, axis=0).astype(BF16)


def forward_kernel(
    owners, experts, buckets,
    x_ref, cot_ref, segment_ref, route_ref, place_ref, in_half_ref, out_half_ref, small_part_ref,
    hidden_ref, normed_ref, triple_ref, context_ref, prob_ref, gate_ref,
    x_rows_ref, gate_rows_ref, cot_rows_ref, in_ref, out_ref, small_ref,
    table_ref, mask_ref, one_ref, half_ref, cot_send_ref, small_got_ref,
    weight_send, weight_recv, cot_send, cot_recv,
):
    me, core = lax.axis_index("expert"), lax.axis_index("dp")
    length, width = x_ref.shape
    heads = 2 * prob_ref.shape[0]
    pair = 2 * (width // heads)
    pairs = heads // 2
    reach = length // 2
    span = reach + BLOCK
    scale = 1.0 / math.sqrt(width // heads)
    slots = x_rows_ref.shape[0]
    capacity = slots // owners
    share = in_half_ref.shape[0]

    def block(index):
        return pl.ds(pl.multiple_of(index * capacity, capacity), capacity)

    mine = pl.ds(pl.multiple_of(core * share, share), share)
    greet(me, core, owners)
    weights = [
        remote(in_half_ref, in_ref.at[mine], weight_send.at[0], weight_recv.at[0], (me, 1 - core)),
        remote(out_half_ref, out_ref.at[mine], weight_send.at[1], weight_recv.at[1], (me, 1 - core)),
        remote(small_part_ref, small_got_ref, weight_send.at[2], weight_recv.at[2], (me, 1 - core)),
    ]
    for copy in weights:
        copy.start()
    in_ref[mine, :] = in_half_ref[...]
    out_ref[mine, :] = out_half_ref[...]
    half_ref[...] = cot_ref[...].astype(BF16)

    def cot_copy(step):
        peer = partner(me, step, owners, 1)
        return remote(
            cot_send_ref.at[block(step)], cot_rows_ref.at[block(step)], cot_send.at[step], cot_recv.at[step], (peer, core)
        )

    def dispatch(step, carry):
        peer = partner(me, step, owners, 1)
        first, second = hot_rows(place_ref, peer * capacity, capacity)
        cot_send_ref[block(step), :] = dot(bf16_of(first | second), half_ref[...]).astype(BF16)

        @pl.when(step >= 2)
        def _():
            cot_copy(step - 1).start()

        return carry

    lax.fori_loop(0, owners, dispatch, 0)
    cot_copy(owners - 1).start()
    cot_rows_ref[block(0), :] = cot_send_ref[block(0), :]

    x = x_ref[...]
    rms = lax.rsqrt(jnp.mean(x * x, axis=1, keepdims=True) + EPS)
    for copy in weights:
        copy.wait_recv()
    small_ref[...] = small_part_ref[...] + small_got_ref[...]
    one_ref[...] = (x * rms * small_ref[experts : experts + 1, :].astype(F32)).astype(BF16)

    chunk = 3 * pair

    def project(step, carry):
        columns = pl.ds(pl.multiple_of(step * chunk, BLOCK), chunk)
        triple_ref[:, columns] = dot(one_ref[...], in_ref[:, columns]).astype(BF16)
        return carry

    lax.fori_loop(0, 3 * width // chunk, project, 0)

    wide = span + BLOCK
    bias = small_ref[experts + 2 : experts + 2 + heads, 0:buckets]
    by_column = dot(bias, bucket_hot(buckets, length, wide).astype(BF16))
    for head in range(heads):
        spread = jnp.broadcast_to(by_column[head : head + 1, :], (BLOCK, wide))
        rolled = pltpu.roll(spread, wide - BLOCK + 1, 1, stride=1, stride_axis=0)
        table_ref[head // 2, (head % 2) * BLOCK : (head % 2 + 1) * BLOCK, :] = rolled[:, :span]

    segment_row = segment_ref[...].astype(F32)
    segment_column = jnp.transpose(jnp.broadcast_to(segment_row, (BLOCK, length)))
    for index, low, high, skip in spans(length):
        rows = index * BLOCK + lax.broadcasted_iota(jnp.int32, (BLOCK, high - low), 0)
        columns = low + lax.broadcasted_iota(jnp.int32, (BLOCK, high - low), 1)
        own = segment_column[index * BLOCK : (index + 1) * BLOCK, 0:1]
        allowed = (rows >= columns) & (own == segment_row[:, low:high])
        mask_ref[index, :, skip:] = jnp.where(allowed, 0.0, MASKED)

    def attend(step, carry):
        base = pl.multiple_of(step * pair, pair)
        query_columns = pl.ds(base, pair)
        key_columns = pl.ds(pl.multiple_of(width + base, pair), pair)
        value_columns = pl.ds(pl.multiple_of(2 * width + base, pair), pair)
        for index, low, high, skip in spans(length):
            rows = slice(index * BLOCK, (index + 1) * BLOCK)
            query = triple_ref[rows, query_columns] * jnp.asarray(scale, BF16)
            stacked = jnp.concatenate(halves(query), axis=0)
            scores = dot(stacked, triple_ref[low:high, key_columns], 1, 1)
            mask = mask_ref[index, :, skip:]
            scores = scores + table_ref[step, :, skip:] + jnp.concatenate([mask, mask], axis=0)
            top = jnp.max(scores, axis=1, keepdims=True)
            weight = jnp.exp(scores - top)
            prob = weight * (1.0 / jnp.sum(weight, axis=1, keepdims=True))
            half = prob.astype(BF16)
            prob_ref[step, index, :, skip:] = half
            first, second = halves(triple_ref[low:high, value_columns])
            context = dot(half[:BLOCK], first) + dot(half[BLOCK:], second)
            context_ref[rows, query_columns] = context.astype(BF16)
        return carry

    lax.fori_loop(0, pairs, attend, 0)

    hidden = x_ref[...] + dot(context_ref[...], out_ref[...])
    hidden_ref[...] = hidden
    rms = lax.rsqrt(jnp.mean(hidden * hidden, axis=1, keepdims=True) + EPS)
    normed = (hidden * rms * small_ref[experts + 1 : experts + 2, :].astype(F32)).astype(BF16)
    normed_ref[...] = normed
    logits = dot(small_ref[0:experts, :], normed, 1, 1)
    expert_ids = lax.broadcasted_iota(jnp.int32, logits.shape, 0)
    first = jnp.sum(jnp.where(expert_ids == route_ref[0:1, :], logits, 0.0), axis=0, keepdims=True)
    second = jnp.sum(jnp.where(expert_ids == route_ref[1:2, :], logits, 0.0), axis=0, keepdims=True)
    gate_first = 1.0 / (1.0 + jnp.exp(second - first))
    gate_second = 1.0 / (1.0 + jnp.exp(first - second))
    gate_ref[0:1, :] = gate_first
    gate_ref[1:2, :] = gate_second
    first_pieces, second_pieces = pieces_of(gate_first), pieces_of(gate_second)

    def outgoing(step, carry):
        first, second = hot_rows(place_ref, step * capacity, capacity)
        x_rows_ref[block(step), :] = dot(bf16_of(first | second), normed_ref[...]).astype(BF16)
        gates = dot(first_pieces, bf16_of(first), 1, 1) + dot(second_pieces, bf16_of(second), 1, 1)
        gate_rows_ref[step] = jnp.sum(gates, axis=0, keepdims=True)
        return carry

    lax.fori_loop(0, owners, outgoing, 0)

    def finish(step, carry):
        cot_copy(step).wait()
        return carry

    lax.fori_loop(1, owners, finish, 0)
    for copy in weights:
        copy.wait_send()


def backward_kernel(
    owners, experts, buckets, digits,
    x_ref, cot_ref, hidden_ref, normed_ref, triple_ref, context_ref, prob_ref, gate_ref, route_ref, place_ref,
    home_ref, dot_ref, in_ref, out_ref, small_ref, y_hbm,
    block_ref, input_grad_ref, in_share_ref, out_share_ref, small_sum_ref,
    context_grad_ref, triple_grad_ref, turned_ref, key_ref, value_ref, diagonal_ref, sums_ref,
    grads_ref, small_mine_ref, small_got_ref, came_ref, work_ref, got_ref, final_ref,
    y_send, y_recv, own_sem, core_send, core_recv, ring_send, ring_recv, small_send, small_recv,
):
    me, core = lax.axis_index("expert"), lax.axis_index("dp")
    hidden_grad_ref = block_ref
    length, width = x_ref.shape
    pairs = prob_ref.shape[0]
    heads = 2 * pairs
    pair = 2 * (width // heads)
    reach = length // 2
    span = reach + BLOCK
    scale = 1.0 / math.sqrt(width // heads)
    slots = home_ref.shape[0]
    capacity = slots // owners

    def block(index):
        return pl.ds(pl.multiple_of(index * capacity, capacity), capacity)

    own_y = pltpu.make_async_copy(y_hbm.at[block(0)], came_ref.at[block(me)], own_sem)
    own_y.start()
    greet(me, core, owners)

    def y_copy(step, sign):
        peer = partner(me, step, owners, -1)
        target = me if sign < 0 else partner(me, step, owners, 1)
        return remote(
            y_hbm.at[block(step)], came_ref.at[block(target)], y_send.at[step], y_recv.at[step], (peer, core)
        )

    def start_y(step, carry):
        y_copy(step, -1).start()
        return carry

    lax.fori_loop(1, owners, start_y, 0)

    def column(row):
        return jnp.transpose(jnp.broadcast_to(row, (BLOCK, length)))

    place_first = column(place_ref[0:1, :].astype(F32))
    place_second = column(place_ref[1:2, :].astype(F32))
    lane = lax.broadcasted_iota(jnp.int32, (length, BLOCK), 1).astype(F32)
    wide_k = 2 * BLOCK

    def hot_columns(group):
        first = (group * BLOCK).astype(F32) if hasattr(group, "astype") else float(group * BLOCK)
        return place_first - first == lane, place_second - first == lane

    def gather_rows(rows_ref, base_ref):
        def add(group, carry):
            left = hot_columns(2 * group)
            right = hot_columns(2 * group + 1)
            hot = jnp.concatenate([bf16_of(left[0] | left[1]), bf16_of(right[0] | right[1])], axis=1)
            rows = pl.ds(pl.multiple_of(group * wide_k, wide_k), wide_k)
            base_ref[...] += dot(hot, rows_ref[rows, :])
            return carry

        lax.fori_loop(0, slots // wide_k, add, 0)

    per_row = BLOCK // capacity

    def dot_row(group):
        if per_row == 1:
            return dot_ref[group]
        return jnp.concatenate([dot_ref[group * per_row + b] for b in range(per_row)], axis=1)

    def pick(group, carry):
        first, second = hot_columns(group)
        row = dot_row(group)
        return carry + jnp.where(first, row, 0.0) - jnp.where(second, row, 0.0)

    picked = lax.fori_loop(0, slots // BLOCK, pick, jnp.zeros((length, BLOCK), F32))
    difference = jnp.sum(picked, axis=1, keepdims=True)
    gates = column(gate_ref[0:1, :]) * column(gate_ref[1:2, :])
    ids = lax.broadcasted_iota(jnp.int32, (length, BLOCK), 1)
    pick_first = jnp.where(column(route_ref[0:1, :].astype(F32)).astype(jnp.int32) == ids, 1.0, 0.0)
    pick_second = jnp.where(column(route_ref[1:2, :].astype(F32)).astype(jnp.int32) == ids, 1.0, 0.0)
    logit_grad = ((pick_first - pick_second) * gates * difference).astype(BF16)

    small_mine_ref[...] = jnp.zeros_like(small_mine_ref)
    hidden_grad_ref[...] = dot(logit_grad[:, 0:experts], small_ref[0:experts, :])
    gather_rows(home_ref, hidden_grad_ref)
    small_mine_ref[0:experts, :] = dot(logit_grad, normed_ref[...], 0, 0)[0:experts, :]

    def settle(step, carry):
        rows = pl.ds(pl.multiple_of(step * BLOCK, BLOCK), BLOCK)
        normed_grad = hidden_grad_ref[rows, :]
        hidden = hidden_ref[rows, :]
        rms = lax.rsqrt(jnp.mean(hidden * hidden, axis=1, keepdims=True) + EPS)
        scaled = normed_grad * small_ref[experts + 1 : experts + 2, :].astype(F32)
        inner = jnp.mean(scaled * hidden, axis=1, keepdims=True)
        hidden_grad_ref[rows, :] = cot_ref[rows, :] + (rms * scaled - hidden * (rms * rms * rms) * inner)
        return carry + jnp.sum(normed_grad * (hidden * rms), axis=0, keepdims=True)

    small_mine_ref[experts + 1 : experts + 2, :] = lax.fori_loop(
        0, length // BLOCK, settle, jnp.zeros((1, width), F32)
    )

    residual = hidden_grad_ref[...].astype(BF16)
    context_grad_ref[...] = dot(residual, out_ref[...], 1, 1).astype(BF16)
    grads_ref[:, 3 * width :] = dot(jnp.transpose(context_ref[...]), residual)
    diagonal_ref[...] = jnp.zeros_like(diagonal_ref)

    def attend(step, carry):
        base = pl.multiple_of(step * pair, pair)
        query_columns = pl.ds(base, pair)
        key_columns = pl.ds(pl.multiple_of(width + base, pair), pair)
        value_columns = pl.ds(pl.multiple_of(2 * width + base, pair), pair)
        key_ref[...] = jnp.zeros_like(key_ref)
        value_ref[...] = jnp.zeros_like(value_ref)
        for index, low, high, skip in spans(length):
            rows = slice(index * BLOCK, (index + 1) * BLOCK)
            query = triple_ref[rows, query_columns] * jnp.asarray(scale, BF16)
            query = jnp.concatenate(halves(query), axis=0)
            grad = jnp.concatenate(halves(context_grad_ref[rows, query_columns]), axis=0)
            half = prob_ref[step, index, :, skip:]
            prob = half.astype(F32)
            prob_grad = dot(grad, triple_ref[low:high, value_columns], 1, 1)
            norm = 1.0 / jnp.sum(prob, axis=1, keepdims=True)
            row_dot = norm * jnp.sum(prob * prob_grad, axis=1, keepdims=True)
            score_grad = (prob * norm) * (prob_grad - row_dot)
            diagonal_ref[step, :, skip:] += score_grad
            score_half = score_grad.astype(BF16)
            first, second = halves(triple_ref[low:high, key_columns])
            query_grad = dot(score_half[:BLOCK], first) + dot(score_half[BLOCK:], second)
            triple_grad_ref[rows, query_columns] = (query_grad * scale).astype(BF16)
            key_ref[low:high, :] += dot(score_half, query, 0, 0)
            value_ref[low:high, :] += dot(half, grad, 0, 0)
        triple_grad_ref[:, key_columns] = key_ref[...].astype(BF16)
        triple_grad_ref[:, value_columns] = value_ref[...].astype(BF16)
        return carry

    lax.fori_loop(0, pairs, attend, 0)

    x = x_ref[...]
    rms = lax.rsqrt(jnp.mean(x * x, axis=1, keepdims=True) + EPS)
    gain = small_ref[experts : experts + 1, :].astype(F32)
    turned_ref[...] = jnp.transpose((x * rms * gain).astype(BF16))
    chunk = 3 * pair

    def weigh(step, carry):
        columns = pl.ds(pl.multiple_of(step * chunk, BLOCK), chunk)
        grads_ref[:, columns] = dot(turned_ref[...], triple_grad_ref[:, columns])
        return carry

    lax.fori_loop(0, 3 * width // chunk, weigh, 0)

    def finish(step, carry):
        rows = pl.ds(pl.multiple_of(step * BLOCK, BLOCK), BLOCK)
        normed_grad = dot(triple_grad_ref[rows, :], in_ref[...], 1, 1)
        part = x_ref[rows, :]
        scaling = lax.rsqrt(jnp.mean(part * part, axis=1, keepdims=True) + EPS)
        scaled = normed_grad * gain
        inner = jnp.mean(scaled * part, axis=1, keepdims=True)
        input_grad_ref[rows, :] = hidden_grad_ref[rows, :] + (
            scaling * scaled - part * (scaling * scaling * scaling) * inner
        )
        return carry + jnp.sum(normed_grad * (part * scaling), axis=0, keepdims=True)

    small_mine_ref[experts : experts + 1, :] = lax.fori_loop(
        0, length // BLOCK, finish, jnp.zeros((1, width), F32)
    )

    wide = span + BLOCK
    row_ids = lax.broadcasted_iota(jnp.int32, (BLOCK, wide), 0)
    for head in range(heads):
        sheet = diagonal_ref[head // 2, (head % 2) * BLOCK : (head % 2 + 1) * BLOCK, :]
        sheet = jnp.concatenate([sheet, jnp.zeros((BLOCK, BLOCK), F32)], axis=1)
        sheet = pltpu.roll(sheet, BLOCK - 1, 1)
        step = 1
        while step < BLOCK:
            sheet = jnp.where((row_ids & step) != 0, pltpu.roll(sheet, wide - step, 1), sheet)
            step *= 2
        sums_ref[head : head + 1, :] = jnp.sum(sheet, axis=0, keepdims=True)
    hot = bucket_hot(buckets, length, wide).astype(BF16)
    rest = sums_ref[...]
    total = jnp.zeros((heads, buckets), F32)
    for _ in range(3):
        piece = rest.astype(BF16)
        total = total + dot(piece, hot, 1, 1)
        rest = rest - piece.astype(F32)
    small_mine_ref[experts + 2 : experts + 2 + heads, 0:buckets] = total

    reduce_grads(
        me, core, digits, grads_ref, in_share_ref, out_share_ref, small_mine_ref, small_got_ref, small_sum_ref,
        work_ref, got_ref, final_ref, core_send, core_recv, ring_send, ring_recv, small_send, small_recv,
    )

    def finish_y(step, carry):
        y_copy(step, -1).wait_send()
        y_copy(step, 1).wait_recv()
        return carry

    own_y.wait()
    lax.fori_loop(1, owners, finish_y, 0)
    block_ref[...] = hidden_ref[...]
    gather_rows(came_ref, block_ref)


COLORS = 4


def reduce_grads(
    me, core, digits, grads_ref, in_share_ref, out_share_ref, small_mine_ref, small_got_ref, small_sum_ref,
    work_ref, got_ref, final_ref, core_send, core_recv, ring_send, ring_recv, small_send, small_recv,
):
    colors, many, rows, columns = work_ref.shape
    share, wide = in_share_ref.shape[0], grads_ref.shape[1]
    width = out_share_ref.shape[1]
    part_rows = share // colors
    down = part_rows // rows
    strides = []
    stride = 1
    for size in digits:
        strides.append(stride)
        stride *= size
    place = [lax.rem(lax.div(me, strides[axis]), digits[axis]) for axis in range(len(digits))]
    orders = [[0, 1, 2], [1, 0, 2]]

    def pieces(side, use):
        for across in range(wide // columns):
            sheet = grads_ref[
                pl.ds(pl.multiple_of(side * share, share), share), across * columns : (across + 1) * columns
            ]
            for color in range(colors):
                for step in range(down):
                    low = color * part_rows + step * rows
                    use(color, across * down + step, sheet[low : low + rows, :])

    def put_give(color, index, value):
        work_ref[color, index] = value.astype(BF16)

    pieces(1 - core, put_give)
    other = (me, 1 - core)
    swap = [
        remote(work_ref, got_ref.at[0], core_send.at[0], core_recv.at[0], other),
        remote(small_mine_ref, small_got_ref.at[0], core_send.at[1], core_recv.at[1], other),
    ]
    for copy in swap:
        copy.start()
    for copy in swap:
        copy.wait()

    def put_work(color, index, value):
        work_ref[color, index] = (value + got_ref[0, color, index].astype(F32)).astype(BF16)

    pieces(core, put_work)
    small_sum_ref[...] = small_mine_ref[...] + small_got_ref[0]

    def peer_of(axis, ahead):
        digit = lax.rem(place[axis] + ahead, digits[axis])
        return digit, (me + (digit - place[axis]) * strides[axis], core)

    levels = []
    for color in range(colors):
        order = orders[color % 2]
        base, extent, landing, seen = jnp.int32(0), many, 0, []
        for axis in order:
            part = extent // digits[axis]
            seen.append((axis, base, part, landing))
            base = base + place[axis] * part
            extent = part
            landing += part * (digits[axis] - 1)
        levels.append(seen)

    def sem_of(color, level, ahead, way):
        return ((color * 3 + level) * 4 + ahead) * 2 + way

    def scatter(color, level):
        axis, base, part, landing = levels[color][level]
        copies = []
        for ahead in range(1, digits[axis]):
            digit, device = peer_of(axis, ahead)
            index = sem_of(color, level, ahead, 0)
            copies.append(
                remote(
                    work_ref.at[color, pl.ds(base + digit * part, part)],
                    got_ref.at[1, color, pl.ds(landing + (ahead - 1) * part, part)],
                    ring_send.at[index], ring_recv.at[index], device,
                )
            )
        return copies

    def scattered(color, level):
        axis, base, part, landing = levels[color][level]
        mine = base + place[axis] * part
        target = final_ref if level == len(digits) - 1 else work_ref

        def add(step, carry):
            value = work_ref[color, mine + step].astype(F32)
            for ahead in range(1, digits[axis]):
                value = value + got_ref[1, color, landing + (ahead - 1) * part + step].astype(F32)
            target[color, mine + step] = value.astype(BF16)
            return carry

        lax.fori_loop(0, part, add, 0)

    def gather(color, level):
        axis, base, part, _ = levels[color][level]
        mine = base + place[axis] * part
        copies = []
        for ahead in range(1, digits[axis]):
            _, device = peer_of(axis, ahead)
            index = sem_of(color, level, ahead, 1)
            copies.append(
                remote(
                    final_ref.at[color, pl.ds(mine, part)], final_ref.at[color, pl.ds(mine, part)],
                    ring_send.at[index], ring_recv.at[index], device,
                )
            )
        return copies

    def small_copies(axis):
        copies = []
        for ahead in range(1, digits[axis]):
            _, device = peer_of(axis, ahead)
            index = sum(digits[:axis]) - axis + ahead
            copies.append(
                remote(small_sum_ref, small_got_ref.at[index], small_send.at[index], small_recv.at[index], device)
            )
        return copies

    depth = len(digits)
    flights = [None] * colors
    small_flight = None
    ticks = 2 * depth + 1
    lags = [0 if color < 2 else 1 for color in range(colors)]
    for tick in range(ticks + max(lags)):
        for color in range(colors):
            step = tick - lags[color]
            if step < 0 or step >= ticks:
                continue
            if flights[color] is not None:
                for copy in flights[color]:
                    copy.wait()
                flights[color] = None
                if step <= depth:
                    scattered(color, step - 1)
            if step < depth:
                flights[color] = scatter(color, step)
            elif step < 2 * depth:
                flights[color] = gather(color, 2 * depth - 1 - step)
            for copy in flights[color] or ():
                copy.start()
        if tick <= depth:
            if small_flight is not None:
                for copy in small_flight:
                    copy.wait()
                value = small_sum_ref[...]
                for ahead in range(1, digits[tick - 1]):
                    value = value + small_got_ref[sum(digits[: tick - 1]) - (tick - 1) + ahead]
                small_sum_ref[...] = value
                small_flight = None
            if tick < depth:
                small_flight = small_copies(tick)
                for copy in small_flight:
                    copy.start()

    for color in range(colors):
        for index in range(many):
            across, step = index // down, index % down
            low = color * part_rows + step * rows
            value = final_ref[color, index].astype(F32)
            if across * columns < 3 * width:
                in_share_ref[low : low + rows, across * columns : (across + 1) * columns] = value
            else:
                left = across * columns - 3 * width
                out_share_ref[low : low + rows, left : left + columns] = value


MESH = pl.DeviceIdType.MESH
GROUP = 4


def partner(me, step, owners, sign):
    groups = owners // GROUP
    outer = lax.rem(lax.div(me, GROUP) + sign * lax.div(step, GROUP) + groups, groups)
    inner = lax.rem(lax.rem(me, GROUP) + sign * lax.rem(step, GROUP) + GROUP, GROUP)
    return outer * GROUP + inner


def greet(me, core, owners):
    barrier = pltpu.get_barrier_semaphore()

    def signal(step, carry):
        pl.semaphore_signal(
            barrier, inc=1, device_id=(partner(me, step, owners, 1), core), device_id_type=MESH
        )
        return carry

    lax.fori_loop(1, owners, signal, 0)
    pl.semaphore_signal(barrier, inc=1, device_id=(me, 1 - core), device_id_type=MESH)
    pl.semaphore_wait(barrier, owners)


def remote(source, target, send, receive, device):
    return pltpu.make_async_remote_copy(
        src_ref=source, dst_ref=target, send_sem=send, recv_sem=receive,
        device_id=device, device_id_type=MESH,
    )


def whole(count):
    return [pl.BlockSpec(memory_space=pltpu.VMEM)] * count


def params(**extra):
    return pltpu.CompilerParams(vmem_limit_bytes=60 * 2**20, **extra)


def forward(x, cot, segments, route_rows, place_rows, in_half, out_half, small_part, owners, experts, buckets, heads):
    length, width = x.shape
    slots = 4 * length
    blocks, span = length // BLOCK, length // 2 + BLOCK
    shape, vmem, dma = jax.ShapeDtypeStruct, pltpu.VMEM, pltpu.SemaphoreType.DMA
    return pl.pallas_call(
        functools.partial(forward_kernel, owners, experts, buckets),
        out_shape=(
            shape((length, width), F32),
            shape((length, width), BF16),
            shape((length, 3 * width), BF16),
            shape((length, width), BF16),
            shape((heads // 2, blocks, 2 * BLOCK, span), BF16),
            shape((2, length), F32),
            shape((slots, width), BF16),
            shape((owners, 1, slots // owners), F32),
            shape((slots, width), BF16),
            shape((2 * in_half.shape[0], 3 * width), BF16),
            shape((2 * out_half.shape[0], width), BF16),
            shape(small_part.shape, BF16),
        ),
        in_specs=whole(8),
        out_specs=tuple(whole(12)),
        scratch_shapes=[
            vmem((heads // 2, 2 * BLOCK, span), F32),
            vmem((blocks, BLOCK, span), F32),
            vmem((length, width), BF16),
            vmem((length, width), BF16),
            vmem((slots, width), BF16),
            vmem(small_part.shape, BF16),
            dma((3,)),
            dma((3,)),
            dma((owners,)),
            dma((owners,)),
        ],
        compiler_params=params(collective_id=0, has_side_effects=True),
        cost_estimate=pl.CostEstimate(
            flops=12 * 10**9, bytes_accessed=2 * 10**7, transcendentals=2 * 10**6
        ),
        name="attention_forward",
    )(x, cot, segments, route_rows, place_rows, in_half, out_half, small_part)


def backward(operands, y_rows, owners, experts, buckets, digits):
    x, probs, small = operands[0], operands[6], operands[14]
    length, width = x.shape
    pairs, blocks, _, span = probs.shape
    slots = operands[10].shape[0]
    share = width // 2
    columns = width // 2
    piece_rows = share // COLORS * 8 // owners
    shape, vmem, dma = jax.ShapeDtypeStruct, pltpu.VMEM, pltpu.SemaphoreType.DMA
    pieces = (COLORS, owners, piece_rows, columns)
    return pl.pallas_call(
        functools.partial(backward_kernel, owners, experts, buckets, digits),
        out_shape=(
            shape((length, width), F32),
            shape((length, width), F32),
            shape((share, 3 * width), F32),
            shape((share, width), F32),
            shape(small.shape, F32),
        ),
        in_specs=whole(15) + [pl.BlockSpec(memory_space=pl.ANY)],
        out_specs=tuple(whole(5)),
        scratch_shapes=[
            vmem((length, width), BF16),
            vmem((length, 3 * width), BF16),
            vmem((width, length), BF16),
            vmem((length, 2 * (width // (2 * pairs))), F32),
            vmem((length, 2 * (width // (2 * pairs))), F32),
            vmem((pairs, 2 * BLOCK, span), F32),
            vmem((2 * pairs, span + BLOCK), F32),
            vmem((width, 4 * width), F32),
            vmem(small.shape, F32),
            vmem((sum(digits) - len(digits) + 1,) + small.shape, F32),
            vmem((slots, width), BF16),
            vmem(pieces, BF16),
            vmem((2,) + pieces, BF16),
            vmem(pieces, BF16),
            dma((owners,)),
            dma((owners,)),
            dma,
            dma((2,)),
            dma((2,)),
            dma((COLORS * 24,)),
            dma((COLORS * 24,)),
            dma((12,)),
            dma((12,)),
        ],
        compiler_params=pltpu.CompilerParams(
            vmem_limit_bytes=67043328, collective_id=2, has_side_effects=True
        ),
        cost_estimate=pl.CostEstimate(
            flops=25 * 10**9, bytes_accessed=3 * 10**7, transcendentals=2 * 10**6
        ),
        name="attention_backward",
    )(*operands, y_rows)


def expert_kernel(
    owners,
    x_ref, gate_ref, cot_ref, up_hbm, down_hbm,
    y_ref, home_ref, dot_ref, up_grad_ref, down_grad_ref,
    up, down, rows, cots, act, pre, out_sum, back_sum, back_rows, y_rows, gates, dots,
    up_ring, down_ring, up_got, down_got, up_out, down_out,
    weight_sem, cot_sem, own_sem, y_sem,
    x_send, x_recv, gate_send, gate_recv, back_send, back_recv, dot_send, dot_recv,
    ring_send, up_recv, down_recv, out_sem,
):
    me, core = lax.axis_index("expert"), lax.axis_index("dp")
    slots, width = rows.shape
    hidden = up.shape[1]
    capacity = slots // owners
    chunk = min(slots, 512)
    per = chunk // capacity
    tile = 256

    def block(index):
        return pl.ds(pl.multiple_of(index * capacity, capacity), capacity)

    load_up = pltpu.make_async_copy(up_hbm, up, weight_sem.at[0])
    load_down = pltpu.make_async_copy(down_hbm, down, weight_sem.at[1])
    load_cots = pltpu.make_async_copy(cot_ref, cots, cot_sem)
    load_up.start()
    load_down.start()
    load_cots.start()
    own_rows = pltpu.make_async_copy(x_ref.at[block(me)], rows.at[block(0)], own_sem.at[0])
    own_rows.start()
    greet(me, core, owners)

    def send_rows(step):
        peer = partner(me, step, owners, 1)
        return (
            remote(x_ref.at[block(peer)], rows.at[block(step)], x_send.at[step], x_recv.at[step], (peer, core)),
            remote(gate_ref.at[peer], gates.at[step], gate_send.at[step], gate_recv.at[step], (peer, core)),
        )

    def start_rows(step, carry):
        for copy in send_rows(step):
            copy.start()
        return carry

    lax.fori_loop(1, owners, start_rows, 0)
    gates[0] = gate_ref[me]

    def send_back(step):
        peer = partner(me, step, owners, -1)
        return (
            remote(back_rows.at[block(step)], home_ref.at[block(me)], back_send.at[step], back_recv.at[step], (peer, core)),
            remote(dots.at[step], dot_ref.at[me], dot_send.at[step], dot_recv.at[step], (peer, core)),
        )

    def get_back(step):
        peer = partner(me, step, owners, 1)
        return (
            remote(back_rows.at[block(step)], home_ref.at[block(peer)], back_send.at[step], back_recv.at[step], (peer, core)),
            remote(dots.at[step], dot_ref.at[peer], dot_send.at[step], dot_recv.at[step], (peer, core)),
        )

    home_own = pltpu.make_async_copy(back_rows.at[block(0)], home_ref.at[block(me)], own_sem.at[1])
    y_copies = []
    for index in range(slots // chunk):
        first = index * per
        part = slice(index * chunk, (index + 1) * chunk)
        if index == 0:
            own_rows.wait()
            load_cots.wait()
            load_up.wait()
            load_down.wait()

        def arrive(step, carry):
            for copy in send_rows(step):
                copy.wait_recv()
            return carry

        lax.fori_loop(max(first, 1), first + per, arrive, 0)
        column = jnp.concatenate(
            [
                jnp.transpose(jnp.broadcast_to(gates[first + b], (BLOCK, capacity)))[:, 0:1]
                for b in range(per)
            ],
            axis=0,
        )
        out_sum[...] = jnp.zeros_like(out_sum)
        back_sum[...] = jnp.zeros_like(back_sum)

        def through(step, carry):
            columns = pl.ds(pl.multiple_of(step * tile, tile), tile)
            before = dot(rows[part, :], up[:, columns])
            act_grad = dot(cots[part, :], down[columns, :], 1, 1)
            chance = normal_cdf(before)
            value = before * chance
            slope = chance + before * (
                jnp.exp(-0.5 * before * before) * (1.0 / math.sqrt(2.0 * math.pi))
            )
            out_sum[...] += dot(value.astype(BF16), down[columns, :])
            act[part, columns] = (value * column).astype(BF16)
            pre_grad = (act_grad * slope * column).astype(BF16)
            pre[part, columns] = pre_grad
            back_sum[...] += dot(pre_grad, up[:, columns], 1, 1)
            return carry

        lax.fori_loop(0, hidden // tile, through, 0)
        back_rows[part, :] = back_sum[...].astype(BF16)
        produced = out_sum[...]
        inner = jnp.sum(produced * cots[part, :].astype(F32), axis=1, keepdims=True)
        spread = jnp.broadcast_to(inner, (chunk, BLOCK))
        for b in range(per):
            turned = jnp.transpose(spread[b * capacity : (b + 1) * capacity, :])
            dots[first + b] = turned[0:1, :]
        if index >= 2:
            y_copies[index - 2].wait()
        y_rows[index % 2] = (produced * column).astype(BF16)
        y_copy = pltpu.make_async_copy(y_rows.at[index % 2], y_ref.at[part], y_sem.at[index % 2])
        y_copy.start()
        y_copies.append(y_copy)

        def start_back(step, carry):
            for copy in send_back(step):
                copy.start()
            return carry

        lax.fori_loop(max(first, 1), first + per, start_back, 0)
        if index == 0:
            home_own.start()
            dot_ref[me] = dots[0]
    for y_copy in y_copies[-2:]:
        y_copy.wait()

    half = hidden // 2
    count = half // tile

    def columns_of(side, step):
        return pl.ds(pl.multiple_of(side * half + step * tile, tile), tile)

    def up_tile(side, step):
        return dot(rows[...], pre[:, columns_of(side, step)], 0, 0)

    def down_tile(side, step):
        return dot(act[:, columns_of(side, step)], cots[...], 0, 0)

    def up_copy(step):
        slot = lax.rem(step, 2)
        return remote(
            up_ring.at[slot], up_got.at[:, columns_of(0, step)], ring_send.at[slot], up_recv.at[step], (me, 1 - core)
        )

    def down_copy(step):
        slot = lax.rem(step, 2)
        return remote(
            down_ring.at[slot], down_got.at[columns_of(0, step), :], ring_send.at[2 + slot], down_recv.at[step], (me, 1 - core)
        )

    def give(step, carry):
        slot = lax.rem(step, 2)

        @pl.when(step >= 2)
        def _():
            up_copy(step - 2).wait_send()
            down_copy(step - 2).wait_send()

        up_ring[slot] = up_tile(1 - core, step).astype(BF16)
        up_copy(step).start()
        down_ring[slot] = down_tile(1 - core, step).astype(BF16)
        down_copy(step).start()
        return carry

    lax.fori_loop(0, count, give, 0)

    def up_write(step):
        slot = lax.rem(step, 2)
        return pltpu.make_async_copy(up_out.at[slot], up_grad_ref.at[:, columns_of(0, step)], out_sem.at[slot])

    def down_write(step):
        slot = lax.rem(step, 2)
        return pltpu.make_async_copy(down_out.at[slot], down_grad_ref.at[columns_of(0, step), :], out_sem.at[2 + slot])

    def take(step, carry):
        slot = lax.rem(step, 2)

        @pl.when(step >= 2)
        def _():
            up_write(step - 2).wait()
            down_write(step - 2).wait()

        mine = up_tile(core, step)
        up_copy(step).wait_recv()
        up_out[slot] = mine + up_got[:, columns_of(0, step)].astype(F32)
        up_write(step).start()
        mine = down_tile(core, step)
        down_copy(step).wait_recv()
        down_out[slot] = mine + down_got[columns_of(0, step), :].astype(F32)
        down_write(step).start()
        return carry

    lax.fori_loop(0, count, take, 0)

    for step in range(max(count - 2, 0), count):
        up_copy(step).wait_send()
        down_copy(step).wait_send()
        up_write(step).wait()
        down_write(step).wait()
    home_own.wait()

    def finish(step, carry):
        for copy in send_rows(step):
            copy.wait_send()
        for copy in send_back(step):
            copy.wait_send()
        for copy in get_back(step):
            copy.wait_recv()
        return carry

    lax.fori_loop(1, owners, finish, 0)


def experts_of(x_rows, gate_rows, cot_rows, up_matrix, down_matrix, owners):
    slots, width = x_rows.shape
    hidden = up_matrix.shape[1]
    capacity = slots // owners
    chunk, tile, half = min(slots, 512), 256, hidden // 2
    count = half // tile
    shape, vmem, dma = jax.ShapeDtypeStruct, pltpu.VMEM, pltpu.SemaphoreType.DMA
    anywhere = pl.BlockSpec(memory_space=pl.ANY)
    near = pl.BlockSpec(memory_space=pltpu.VMEM)
    return pl.pallas_call(
        functools.partial(expert_kernel, owners),
        out_shape=(
            shape((slots, width), BF16),
            shape((slots, width), BF16),
            shape((owners, 1, capacity), F32),
            shape((width, half), F32),
            shape((half, width), F32),
        ),
        in_specs=[anywhere, near, anywhere, anywhere, anywhere],
        out_specs=(anywhere, anywhere, near, anywhere, anywhere),
        scratch_shapes=[
            vmem((width, hidden), BF16),
            vmem((hidden, width), BF16),
            vmem((slots, width), BF16),
            vmem((slots, width), BF16),
            vmem((slots, hidden), BF16),
            vmem((slots, hidden), BF16),
            vmem((chunk, width), F32),
            vmem((chunk, width), F32),
            vmem((slots, width), BF16),
            vmem((2, chunk, width), BF16),
            vmem((owners, 1, capacity), F32),
            vmem((owners, 1, capacity), F32),
            vmem((2, width, tile), BF16),
            vmem((2, tile, width), BF16),
            vmem((width, half), BF16),
            vmem((half, width), BF16),
            vmem((2, width, tile), F32),
            vmem((2, tile, width), F32),
            dma((2,)),
            dma,
            dma((2,)),
            dma((2,)),
        ]
        + [dma((owners,))] * 8
        + [dma((4,)), dma((count,)), dma((count,)), dma((4,))],
        compiler_params=pltpu.CompilerParams(
            vmem_limit_bytes=67043328, collective_id=1, has_side_effects=True
        ),
        cost_estimate=pl.CostEstimate(
            flops=58 * 10**9, bytes_accessed=4 * 10**7, transcendentals=2 * 10**7
        ),
        name="experts",
    )(x_rows, gate_rows, cot_rows, up_matrix, down_matrix)


def shards(
    block_input,
    cotangent,
    segment_ids,
    routes,
    slot_ids,
    attention_in,
    attention_out,
    router_weight,
    first_gain,
    second_gain,
    bias_table,
    expert_up,
    expert_down,
):
    length, width = block_input.shape
    owners = lax.axis_size("expert")
    capacity = 4 * length // owners
    experts = router_weight.shape[1]
    heads = bias_table.shape[1]
    member = lax.axis_index("dp")
    pair_size = lax.axis_size("dp")
    buckets = pair_size * bias_table.shape[0]
    share = width // pair_size
    inner = owners // 4
    side = math.isqrt(inner)
    digits = (side, inner // side, 4)

    rows = -(-(experts + 2 + heads) // 16) * 16
    wide_part = jnp.concatenate([router_weight.T, first_gain[None], second_gain[None]], axis=0)
    small_part = jnp.zeros((rows, width), BF16)
    small_part = lax.dynamic_update_slice(small_part, wide_part, (0, member * share))
    small_part = lax.dynamic_update_slice(
        small_part, bias_table.T, (experts + 2, member * bias_table.shape[0])
    )
    route_rows = routes.T
    place_rows = route_rows * capacity + slot_ids.T
    (
        hidden_state, normed_two, triple, context, probs, gates,
        x_rows, gate_rows, cot_rows, full_in, full_out, small,
    ) = forward(
        block_input, cotangent, segment_ids, route_rows, place_rows, attention_in, attention_out, small_part,
        owners, experts, buckets, heads,
    )
    y_rows, home_rows, gate_dots, up_share, down_share = experts_of(
        x_rows, gate_rows, cot_rows, expert_up[0], expert_down[0], owners
    )
    block_output, input_grad, in_share, out_share, small_sum = backward(
        (
            block_input, cotangent, hidden_state, normed_two, triple, context, probs, gates, route_rows, place_rows,
            home_rows, gate_dots, full_in, full_out, small,
        ),
        y_rows, owners, experts, buckets, digits,
    )
    mine = lax.dynamic_slice_in_dim(small_sum[: experts + 2], member * share, share, 1)
    bias_grad = lax.dynamic_slice(
        small_sum, (experts + 2, member * bias_table.shape[0]), (heads, bias_table.shape[0])
    )
    return (
        block_output,
        input_grad,
        in_share,
        out_share,
        mine[:experts].T,
        mine[experts],
        mine[experts + 1],
        bias_grad.T,
        up_share[None],
        down_share[None],
    )


def solution(mesh):
    rows = P(("expert", "dp"), None)
    return jax.shard_map(
        shards,
        mesh=mesh,
        in_specs=(
            rows,
            rows,
            rows,
            rows,
            rows,
            P("dp", None),
            P("dp", None),
            P("dp", None),
            P("dp"),
            P("dp"),
            P("dp", None),
            P("expert", None, None),
            P("expert", None, None),
        ),
        out_specs=(
            rows,
            rows,
            P("dp", None),
            P("dp", None),
            P("dp", None),
            P("dp"),
            P("dp"),
            P("dp", None),
            P("expert", None, "dp"),
            P("expert", "dp", None),
        ),
        check_vma=False,
    )
```

time: 739 us -> 433 us (0.59); the launches traced: 728 us -> 431 us
  waiting for transfers between devices: 420 us -> 0 us
  Pallas kernels: 56.8 us -> 407 us
  matrix products: 121 us -> 0 us
  blocking collectives: 48.4 us -> 0 us
  starting transfers between devices: 29.1 us -> 0 us
  other arithmetic: 24.6 us -> 2.04 us
  between operations: 14.8 us -> 0.73 us
  local copies, waits for them, and re-layouts: 12.4 us -> 21.1 us
    pallas_call x2 -> x3, Pallas kernels: 56.8 us -> 407 us  [the longest x1 176 us: backward(): pl.pallas_call(functools.partial(backward_kernel, owners, experts, bucket...]
    all_to_all x5 -> x0, waiting for transfers between devices: 253 us -> none  [exchange(): lax.all_to_all(rows.reshape(owners, -1, rows.shape[-1]), 'expert', split_...]
    psum x1 -> x0, waiting for transfers between devices: 148 us -> none  [shards(): lax.psum(lax.psum_scatter(big, 'dp', scatter_dimension=0, tiled=True), 'e...]
    dot_general x13 -> x0, matrix products: 121 us -> none  [dot(): lax.dot_general(left, right, (((left_dim,), (right_dim,)), ((), ())), pre...]
    psum x1 -> x0, blocking collectives: 41.4 us -> none  [shards(): lax.psum((router_grad, first_grad[0], second_grad, bias_grad), ('expert',...]
    all_to_all x5 -> x0, starting transfers between devices: 28.8 us -> none  [exchange(): lax.all_to_all(rows.reshape(owners, -1, rows.shape[-1]), 'expert', split_...]
    all_gather x2 -> x0, waiting for transfers between devices: 17.2 us -> none  [the longest x1 15.5 us: shards(): lax.all_gather(attention_in, 'dp', axis=0, tiled=True)]
    unnamed x28 -> x24, local copies, waits for them, and re-layouts: 0.64 us -> 15.4 us
  transfers between devices with their start and end apart: 11 -> 0, of which waited for: 8 -> 0; matrix products, arithmetic and copies ran while one was open for 11% -> 0% of each run, Pallas kernels for 0% -> 0%
where the time goes in v1:
time: 433 us; the launch traced here: 431 us
  Pallas kernels  407 us (94%)
  local copies, waits for them, and re-layouts  21.1 us (5%)
    pallas_call x1, Pallas kernels, backward(): pl.pallas_call(functools.partial(backward_kernel, owners, experts, bucket...  176 us
    pallas_call x1, Pallas kernels, experts_of(): pl.pallas_call(functools.partial(expert_kernel, owners), out_shape=(shape...  145 us
    pallas_call x1, Pallas kernels, forward(): pl.pallas_call(functools.partial(forward_kernel, owners, experts, buckets...  85.8 us
    unnamed x24, local copies, waits for them, and re-layouts  15.4 us

profile of v1, /device:TPU:12, one launch (start us, length us, event | category | flops | bytes accessed | tf_op | source)
XLA Modules:
  0.0 430.7 jit_solution(5869945300891862194)
XLA Ops:
  0.6 0.7 broadcast_in_dim.16
  1.3 0.7 broadcast_in_dim.17
  2.0 0.7 pad_maximum_fusion
  2.7 1.0 dynamic_update_slice.6
  3.7 0.8 copy.23
  4.5 0.3 dynamic_update_slice.7.small_part_ref
  4.9 1.3 bitcast_add_fusion.place_ref
  6.2 85.8 %attention_forward.1 = (f32[512,768]{1,0:T(8,128)}, bf16[512,768]{1,0:T(8,128)(2,1)}, bf16[512,2304]{1,0:T(8,128)(2,1)}, bf16[512,768]{1,0:T(8,128)(2,1)}, bf16[...) custom-call(f32[512,768]{1,0:T(8,128)} %x_ref.3, ...), custom_call_target="tpu_custom_call" | custom-call | flops 12000000000 | bytes 20000000 | tf_op jit(solution)/shard_map/attention_forward/pallas_call | solution.py:654
  92.0 145.0 %experts.1 = (bf16[2048,768]{1,0:T(8,128)(2,1)}, bf16[2048,768]{1,0:T(8,128)(2,1)}, f32[16,1,128]{2,1,0:T(1,128)}, f32[768,1536]{1,0:T(8,128)}, f32[1536,768]{1,0:T(8,128)}) custom-call(bf16[2048,768]{1,0:T(8,128)(2,1)} %get-tuple-element.38.x_ref, f32[16,1,128]{2,1,0:T(1,128)} %get-tuple-element.39.gate_ref, bf16[2048,768]{1,0:T(8,128)(2,1)} %get-tuple-element.40.cot_ref, ...), custom_call_target="tpu_custom_call" | custom-call | flops 57999998976 | bytes 40000000 | tf_op jit(solution)/shard_map/experts/pallas_call | solution.py:974
  237.0 176.1 %attention_backward.1 = (f32[512,768]{1,0:T(8,128)}, f32[512,768]{1,0:T(8,128)}, f32[384,2304]{1,0:T(8,128)}, f32[384,768]{1,0:T(8,128)}, f32[32,768]{1,0:T(8,128)}) custom-call(f32[512,768]{1,0:T(8,128)} %x_ref.3, f32[512,768]{1,0:T(8,128)} %cot_ref.3, f32[512,768]{1,0:T(8,128)} %get-tuple-element.32.hidden_ref, ...), custom_call_target="tpu_custom_call" | custom-call | flops 24999999488 | bytes 30000000 | tf_op jit(solution)/shard_map/attention_backward/pallas_call | solution.py:702
  413.0 1.0 slice.12
  414.1 0.6 dynamic-slice_bitcast_fusion
  414.7 0.7 dynamic-slice_reduce_fusion
  415.3 0.8 dynamic-slice_bitcast_fusion.1
  416.1 0.7 copy.24
  416.8 2.8 copy.33
  419.6 1.1 copy.34
  420.8 1.8 copy.35
  422.6 1.4 copy-done.2
  424.0 1.0 copy.36
  425.0 2.4 copy.37
  427.4 0.8 slice-done
  428.2 0.3 slice-done.1
  428.5 2.2 copy.38
  (16 shorter events, 0.0 us)
Async XLA Ops:
  4.8 1.3 copy-start.3
  413.0 6.6 %copy-start.1 = (f32[512,768]{1,0:T(8,128)S(1)}, f32[512,768]{1,0:T(8,128)}, u32[]{:S(2)}) copy-start(f32[512,768]{1,0:T(8,128)} %get-tuple-element.77) | copy-start | bytes 4718596
  416.8 4.0 copy-start
  419.6 5.4 %slice-start.2 = ((s8[4718592]{0:T(1024)(128)(4,1)}), s8[4194304]{0:T(1024)(128)(4,1)S(1)}, s32[]{:S(2)}) async-start(s8[4718592]{0:T(1024)(128)(4,1)} %bitcast.17), calls=%async_computation.2 | async-start | bytes 8388608
  420.7 3.2 copy-start.2
  420.7 4.2 slice-start.3
  424.0 4.3 slice-start
  425.0 3.5 slice-start.1

commit v2 on v1

--- a/solution.py
+++ b/solution.py
@@ -87,8 +87,9 @@
 def forward_kernel(
     owners, experts, buckets,
     x_ref, cot_ref, segment_ref, route_ref, place_ref, in_half_ref, out_half_ref, small_part_ref,
-    hidden_ref, normed_ref, triple_ref, context_ref, prob_ref, gate_ref,
-    x_rows_ref, gate_rows_ref, cot_rows_ref, in_ref, out_ref, small_ref,
+    hidden_hbm, normed_hbm, triple_hbm, context_hbm, prob_hbm, gate_ref,
+    x_rows_hbm, gate_rows_ref, cot_rows_ref, in_hbm, out_hbm, small_ref,
+    hidden_ref, normed_ref, triple_ref, context_ref, prob_ref, x_rows_ref, in_ref, out_ref, store_sem,
     table_ref, mask_ref, one_ref, half_ref, cot_send_ref, small_got_ref,
     weight_send, weight_recv, cot_send, cot_recv,
 ):
@@ -107,7 +108,15 @@
     def block(index):
         return pl.ds(pl.multiple_of(index * capacity, capacity), capacity)
 
+    stores = []
+
+    def store(source, target):
+        copy = pltpu.make_async_copy(source, target, store_sem.at[len(stores)])
+        copy.start()
+        stores.append(copy)
+
     mine = pl.ds(pl.multiple_of(core * share, share), share)
+    half_ref[...] = cot_ref[...].astype(BF16)
     greet(me, core, owners)
     weights = [
         remote(in_half_ref, in_ref.at[mine], weight_send.at[0], weight_recv.at[0], (me, 1 - core)),
@@ -118,7 +127,6 @@
         copy.start()
     in_ref[mine, :] = in_half_ref[...]
     out_ref[mine, :] = out_half_ref[...]
-    half_ref[...] = cot_ref[...].astype(BF16)
 
     def cot_copy(step):
         peer = partner(me, step, owners, 1)
@@ -139,13 +147,15 @@
 
     lax.fori_loop(0, owners, dispatch, 0)
     cot_copy(owners - 1).start()
-    cot_rows_ref[block(0), :] = cot_send_ref[block(0), :]
+    store(cot_send_ref.at[block(0)], cot_rows_ref.at[block(0)])
 
     x = x_ref[...]
     rms = lax.rsqrt(jnp.mean(x * x, axis=1, keepdims=True) + EPS)
     for copy in weights:
         copy.wait_recv()
     small_ref[...] = small_part_ref[...] + small_got_ref[...]
+    store(in_ref, in_hbm)
+    store(out_ref, out_hbm)
     one_ref[...] = (x * rms * small_ref[experts : experts + 1, :].astype(F32)).astype(BF16)
 
     chunk = 3 * pair
@@ -157,6 +167,7 @@
 
     lax.fori_loop(0, 3 * width // chunk, project, 0)
 
+    store(triple_ref, triple_hbm)
     wide = span + BLOCK
     bias = small_ref[experts + 2 : experts + 2 + heads, 0:buckets]
     by_column = dot(bias, bucket_hot(buckets, length, wide).astype(BF16))
@@ -197,12 +208,16 @@
         return carry
 
     lax.fori_loop(0, pairs, attend, 0)
+    store(prob_ref, prob_hbm)
+    store(context_ref, context_hbm)
 
     hidden = x_ref[...] + dot(context_ref[...], out_ref[...])
     hidden_ref[...] = hidden
+    store(hidden_ref, hidden_hbm)
     rms = lax.rsqrt(jnp.mean(hidden * hidden, axis=1, keepdims=True) + EPS)
     normed = (hidden * rms * small_ref[experts + 1 : experts + 2, :].astype(F32)).astype(BF16)
     normed_ref[...] = normed
+    store(normed_ref, normed_hbm)
     logits = dot(small_ref[0:experts, :], normed, 1, 1)
     expert_ids = lax.broadcasted_iota(jnp.int32, logits.shape, 0)
     first = jnp.sum(jnp.where(expert_ids == route_ref[0:1, :], logits, 0.0), axis=0, keepdims=True)
@@ -221,6 +236,7 @@
         return carry
 
     lax.fori_loop(0, owners, outgoing, 0)
+    store(x_rows_ref, x_rows_hbm)
 
     def finish(step, carry):
         cot_copy(step).wait()
@@ -229,13 +245,16 @@
     lax.fori_loop(1, owners, finish, 0)
     for copy in weights:
         copy.wait_send()
+    for copy in stores:
+        copy.wait()
 
 
 def backward_kernel(
     owners, experts, buckets, digits,
-    x_ref, cot_ref, hidden_ref, normed_ref, triple_ref, context_ref, prob_ref, gate_ref, route_ref, place_ref,
-    home_ref, dot_ref, in_ref, out_ref, small_ref, y_hbm,
+    x_hbm, cot_hbm, hidden_hbm, normed_hbm, triple_hbm, context_hbm, prob_hbm, gate_ref, route_ref, place_ref,
+    home_hbm, dot_ref, in_hbm, out_hbm, small_ref, y_hbm,
     block_ref, input_grad_ref, in_share_ref, out_share_ref, small_sum_ref,
+    home_ref, cot_ref, hidden_ref, normed_ref, context_ref, out_ref, x_ref, triple_ref, prob_ref, in_ref, load_sem,
     context_grad_ref, triple_grad_ref, turned_ref, key_ref, value_ref, diagonal_ref, sums_ref,
     grads_ref, small_mine_ref, small_got_ref, came_ref, work_ref, got_ref, final_ref,
     y_send, y_recv, own_sem, core_send, core_recv, ring_send, ring_recv, small_send, small_recv,
@@ -255,6 +274,25 @@
     def block(index):
         return pl.ds(pl.multiple_of(index * capacity, capacity), capacity)
 
+    loads = [
+        pltpu.make_async_copy(source, target, load_sem.at[index])
+        for index, (source, target) in enumerate(
+            (
+                (home_hbm, home_ref),
+                (cot_hbm, cot_ref),
+                (hidden_hbm, hidden_ref),
+                (normed_hbm, normed_ref),
+                (context_hbm, context_ref),
+                (out_hbm, out_ref),
+                (x_hbm, x_ref),
+                (triple_hbm, triple_ref),
+                (prob_hbm, prob_ref),
+                (in_hbm, in_ref),
+            )
+        )
+    ]
+    for copy in loads:
+        copy.start()
     own_y = pltpu.make_async_copy(y_hbm.at[block(0)], came_ref.at[block(me)], own_sem)
     own_y.start()
     greet(me, core, owners)
@@ -316,6 +354,8 @@
     logit_grad = ((pick_first - pick_second) * gates * difference).astype(BF16)
 
     small_mine_ref[...] = jnp.zeros_like(small_mine_ref)
+    for copy in loads[:6]:
+        copy.wait()
     hidden_grad_ref[...] = dot(logit_grad[:, 0:experts], small_ref[0:experts, :])
     gather_rows(home_ref, hidden_grad_ref)
     small_mine_ref[0:experts, :] = dot(logit_grad, normed_ref[...], 0, 0)[0:experts, :]
@@ -335,9 +375,20 @@
     )
 
     residual = hidden_grad_ref[...].astype(BF16)
+    grads_ref[:, 3 * width :] = dot(jnp.transpose(context_ref[...]), residual)
+    advance, advance_small = reducer(
+        me, core, digits, grads_ref, in_share_ref, out_share_ref, small_mine_ref, small_got_ref, small_sum_ref,
+        work_ref, got_ref, final_ref, core_send, core_recv, ring_send, ring_recv, small_send, small_recv,
+    )
+    advance(3)
     context_grad_ref[...] = dot(residual, out_ref[...], 1, 1).astype(BF16)
-    grads_ref[:, 3 * width :] = dot(jnp.transpose(context_ref[...]), residual)
     diagonal_ref[...] = jnp.zeros_like(diagonal_ref)
+    for copy in loads[6:]:
+        copy.wait()
+    x = x_ref[...]
+    rms = lax.rsqrt(jnp.mean(x * x, axis=1, keepdims=True) + EPS)
+    gain = small_ref[experts : experts + 1, :].astype(F32)
+    turned_ref[...] = jnp.transpose((x * rms * gain).astype(BF16))
 
     def attend(step, carry):
         base = pl.multiple_of(step * pair, pair)
@@ -368,20 +419,21 @@
         triple_grad_ref[:, value_columns] = value_ref[...].astype(BF16)
         return carry
 
-    lax.fori_loop(0, pairs, attend, 0)
-
-    x = x_ref[...]
-    rms = lax.rsqrt(jnp.mean(x * x, axis=1, keepdims=True) + EPS)
-    gain = small_ref[experts : experts + 1, :].astype(F32)
-    turned_ref[...] = jnp.transpose((x * rms * gain).astype(BF16))
-    chunk = 3 * pair
-
-    def weigh(step, carry):
-        columns = pl.ds(pl.multiple_of(step * chunk, BLOCK), chunk)
-        grads_ref[:, columns] = dot(turned_ref[...], triple_grad_ref[:, columns])
-        return carry
-
-    lax.fori_loop(0, 3 * width // chunk, weigh, 0)
+    groups = COLORS - 1
+    part = width // groups
+    for group in range(groups):
+        lax.fori_loop(group * pairs // groups, (group + 1) * pairs // groups, attend, 0)
+        for color in [3, *range(group)]:
+            advance(color)
+
+        def weigh(section, carry):
+            source = pl.ds(pl.multiple_of(section * width + group * part, BLOCK), part)
+            target = pl.ds(pl.multiple_of(group * width + section * part, BLOCK), part)
+            grads_ref[:, target] = dot(turned_ref[...], triple_grad_ref[:, source])
+            return carry
+
+        lax.fori_loop(0, 3, weigh, 0)
+        advance(group)
 
     def finish(step, carry):
         rows = pl.ds(pl.multiple_of(step * BLOCK, BLOCK), BLOCK)
@@ -399,6 +451,8 @@
         0, length // BLOCK, finish, jnp.zeros((1, width), F32)
     )
 
+    for color in (2, 1, 0, 3):
+        advance(color)
     wide = span + BLOCK
     row_ids = lax.broadcasted_iota(jnp.int32, (BLOCK, wide), 0)
     for head in range(heads):
@@ -419,34 +473,34 @@
         rest = rest - piece.astype(F32)
     small_mine_ref[experts + 2 : experts + 2 + heads, 0:buckets] = total
 
-    reduce_grads(
-        me, core, digits, grads_ref, in_share_ref, out_share_ref, small_mine_ref, small_got_ref, small_sum_ref,
-        work_ref, got_ref, final_ref, core_send, core_recv, ring_send, ring_recv, small_send, small_recv,
-    )
-
     def finish_y(step, carry):
         y_copy(step, -1).wait_send()
         y_copy(step, 1).wait_recv()
         return carry
 
-    own_y.wait()
-    lax.fori_loop(1, owners, finish_y, 0)
-    block_ref[...] = hidden_ref[...]
-    gather_rows(came_ref, block_ref)
+    for turn in range(2 * len(digits) + 2):
+        for color in (2, 1, 0, 3):
+            advance(color)
+        advance_small()
+        if turn == 3:
+            own_y.wait()
+            lax.fori_loop(1, owners, finish_y, 0)
+            block_ref[...] = hidden_ref[...]
+            gather_rows(came_ref, block_ref)
 
 
 COLORS = 4
 
 
-def reduce_grads(
+def reducer(
     me, core, digits, grads_ref, in_share_ref, out_share_ref, small_mine_ref, small_got_ref, small_sum_ref,
     work_ref, got_ref, final_ref, core_send, core_recv, ring_send, ring_recv, small_send, small_recv,
 ):
-    colors, many, rows, columns = work_ref.shape
-    share, wide = in_share_ref.shape[0], grads_ref.shape[1]
-    width = out_share_ref.shape[1]
-    part_rows = share // colors
-    down = part_rows // rows
+    _, many, rows, columns = work_ref.shape
+    share, width = out_share_ref.shape
+    groups = COLORS - 1
+    section = width // groups
+    down = share // rows
     strides = []
     stride = 1
     for size in digits:
@@ -454,43 +508,45 @@
         stride *= size
     place = [lax.rem(lax.div(me, strides[axis]), digits[axis]) for axis in range(len(digits))]
     orders = [[0, 1, 2], [1, 0, 2]]
-
-    def pieces(side, use):
-        for across in range(wide // columns):
+    other = (me, 1 - core)
+
+    def sheets(color, side):
+        for across in range(width // columns):
             sheet = grads_ref[
-                pl.ds(pl.multiple_of(side * share, share), share), across * columns : (across + 1) * columns
+                pl.ds(pl.multiple_of(side * share, share), share),
+                color * width + across * columns : color * width + (across + 1) * columns,
             ]
-            for color in range(colors):
-                for step in range(down):
-                    low = color * part_rows + step * rows
-                    use(color, across * down + step, sheet[low : low + rows, :])
-
-    def put_give(color, index, value):
-        work_ref[color, index] = value.astype(BF16)
-
-    pieces(1 - core, put_give)
-    other = (me, 1 - core)
-    swap = [
-        remote(work_ref, got_ref.at[0], core_send.at[0], core_recv.at[0], other),
-        remote(small_mine_ref, small_got_ref.at[0], core_send.at[1], core_recv.at[1], other),
-    ]
-    for copy in swap:
-        copy.start()
-    for copy in swap:
-        copy.wait()
-
-    def put_work(color, index, value):
-        work_ref[color, index] = (value + got_ref[0, color, index].astype(F32)).astype(BF16)
-
-    pieces(core, put_work)
-    small_sum_ref[...] = small_mine_ref[...] + small_got_ref[0]
+            for step in range(down):
+                yield across * down + step, sheet[step * rows : (step + 1) * rows, :]
+
+    def swap(color):
+        for index, value in sheets(color, 1 - core):
+            work_ref[color, index] = value.astype(BF16)
+        return [remote(work_ref.at[color], got_ref.at[0, color], core_send.at[color], core_recv.at[color], other)]
+
+    def swapped(color):
+        for index, value in sheets(color, core):
+            work_ref[color, index] = (value + got_ref[0, color, index].astype(F32)).astype(BF16)
+
+    def settled(color):
+        for index in range(many):
+            across, step = index // down, index % down
+            low = step * rows
+            value = final_ref[color, index].astype(F32)
+            if color == groups:
+                out_share_ref[low : low + rows, across * columns : (across + 1) * columns] = value
+                continue
+            for left in range(0, columns, BLOCK):
+                start = across * columns + left
+                target = start // section * width + color * section + start % section
+                in_share_ref[low : low + rows, target : target + BLOCK] = value[:, left : left + BLOCK]
 
     def peer_of(axis, ahead):
         digit = lax.rem(place[axis] + ahead, digits[axis])
         return digit, (me + (digit - place[axis]) * strides[axis], core)
 
     levels = []
-    for color in range(colors):
+    for color in range(COLORS):
         order = orders[color % 2]
         base, extent, landing, seen = jnp.int32(0), many, 0, []
         for axis in order:
@@ -559,51 +615,62 @@
         return copies
 
     depth = len(digits)
-    flights = [None] * colors
-    small_flight = None
-    ticks = 2 * depth + 1
-    lags = [0 if color < 2 else 1 for color in range(colors)]
-    for tick in range(ticks + max(lags)):
-        for color in range(colors):
-            step = tick - lags[color]
-            if step < 0 or step >= ticks:
-                continue
-            if flights[color] is not None:
-                for copy in flights[color]:
-                    copy.wait()
-                flights[color] = None
-                if step <= depth:
-                    scattered(color, step - 1)
-            if step < depth:
-                flights[color] = scatter(color, step)
-            elif step < 2 * depth:
-                flights[color] = gather(color, 2 * depth - 1 - step)
-            for copy in flights[color] or ():
-                copy.start()
-        if tick <= depth:
-            if small_flight is not None:
-                for copy in small_flight:
-                    copy.wait()
-                value = small_sum_ref[...]
-                for ahead in range(1, digits[tick - 1]):
-                    value = value + small_got_ref[sum(digits[: tick - 1]) - (tick - 1) + ahead]
-                small_sum_ref[...] = value
-                small_flight = None
-            if tick < depth:
-                small_flight = small_copies(tick)
-                for copy in small_flight:
-                    copy.start()
-
-    for color in range(colors):
-        for index in range(many):
-            across, step = index // down, index % down
-            low = color * part_rows + step * rows
-            value = final_ref[color, index].astype(F32)
-            if across * columns < 3 * width:
-                in_share_ref[low : low + rows, across * columns : (across + 1) * columns] = value
-            else:
-                left = across * columns - 3 * width
-                out_share_ref[low : low + rows, left : left + columns] = value
+    stage, flight = [0] * COLORS, [()] * COLORS
+
+    def advance(color):
+        now = stage[color]
+        if now > 2 * depth + 1:
+            return
+        for copy in flight[color]:
+            copy.wait()
+        if now == 1:
+            swapped(color)
+        elif 1 < now <= depth + 1:
+            scattered(color, now - 2)
+        elif now == 2 * depth + 1:
+            settled(color)
+        if now == 0:
+            flight[color] = swap(color)
+        elif now <= depth:
+            flight[color] = scatter(color, now - 1)
+        elif now <= 2 * depth:
+            flight[color] = gather(color, 2 * depth - now)
+        else:
+            flight[color] = ()
+        for copy in flight[color]:
+            copy.start()
+        stage[color] = now + 1
+
+    small_state = [0, ()]
+
+    def advance_small():
+        now, flying = small_state
+        if now > depth + 1:
+            return
+        for copy in flying:
+            copy.wait()
+        if now == 1:
+            small_sum_ref[...] = small_mine_ref[...] + small_got_ref[0]
+        elif now > 1:
+            value = small_sum_ref[...]
+            for ahead in range(1, digits[now - 2]):
+                value = value + small_got_ref[sum(digits[: now - 2]) - (now - 2) + ahead]
+            small_sum_ref[...] = value
+        if now == 0:
+            flying = [
+                remote(
+                    small_mine_ref, small_got_ref.at[0], core_send.at[COLORS], core_recv.at[COLORS], other
+                )
+            ]
+        elif now <= depth:
+            flying = small_copies(now - 1)
+        else:
+            flying = ()
+        for copy in flying:
+            copy.start()
+        small_state[:] = now + 1, flying
+
+    return advance, advance_small
 
 
 MESH = pl.DeviceIdType.MESH
@@ -650,6 +717,7 @@
     length, width = x.shape
     slots = 4 * length
     blocks, span = length // BLOCK, length // 2 + BLOCK
+    any_, near = pl.BlockSpec(memory_space=pl.ANY), pl.BlockSpec(memory_space=pltpu.VMEM)
     shape, vmem, dma = jax.ShapeDtypeStruct, pltpu.VMEM, pltpu.SemaphoreType.DMA
     return pl.pallas_call(
         functools.partial(forward_kernel, owners, experts, buckets),
@@ -668,8 +736,17 @@
             shape(small_part.shape, BF16),
         ),
         in_specs=whole(8),
-        out_specs=tuple(whole(12)),
+        out_specs=(any_, any_, any_, any_, any_, near, any_, near, any_, any_, any_, near),
         scratch_shapes=[
+            vmem((length, width), F32),
+            vmem((length, width), BF16),
+            vmem((length, 3 * width), BF16),
+            vmem((length, width), BF16),
+            vmem((heads // 2, blocks, 2 * BLOCK, span), BF16),
+            vmem((slots, width), BF16),
+            vmem((2 * in_half.shape[0], 3 * width), BF16),
+            vmem((2 * out_half.shape[0], width), BF16),
+            dma((9,)),
             vmem((heads // 2, 2 * BLOCK, span), F32),
             vmem((blocks, BLOCK, span), F32),
             vmem((length, width), BF16),
@@ -696,7 +773,8 @@
     slots = operands[10].shape[0]
     share = width // 2
     columns = width // 2
-    piece_rows = share // COLORS * 8 // owners
+    piece_rows = share * 2 // owners
+    any_, near = pl.BlockSpec(memory_space=pl.ANY), pl.BlockSpec(memory_space=pltpu.VMEM)
     shape, vmem, dma = jax.ShapeDtypeStruct, pltpu.VMEM, pltpu.SemaphoreType.DMA
     pieces = (COLORS, owners, piece_rows, columns)
     return pl.pallas_call(
@@ -708,9 +786,20 @@
             shape((share, width), F32),
             shape(small.shape, F32),
         ),
-        in_specs=whole(15) + [pl.BlockSpec(memory_space=pl.ANY)],
+        in_specs=[any_] * 7 + [near] * 3 + [any_, near, any_, any_, near, any_],
         out_specs=tuple(whole(5)),
         scratch_shapes=[
+            vmem((slots, width), BF16),
+            vmem((length, width), F32),
+            vmem((length, width), F32),
+            vmem((length, width), BF16),
+            vmem((length, width), BF16),
+            vmem((width, width), BF16),
+            vmem((length, width), F32),
+            vmem((length, 3 * width), BF16),
+            vmem(probs.shape, BF16),
+            vmem((width, 3 * width), BF16),
+            dma((10,)),
             vmem((length, width), BF16),
             vmem((length, 3 * width), BF16),
             vmem((width, length), BF16),
@@ -728,8 +817,8 @@
             dma((owners,)),
             dma((owners,)),
             dma,
-            dma((2,)),
-            dma((2,)),
+            dma((COLORS + 1,)),
+            dma((COLORS + 1,)),
             dma((COLORS * 24,)),
             dma((COLORS * 24,)),
             dma((12,)),
@@ -788,7 +877,8 @@
             copy.start()
         return carry
 
-    lax.fori_loop(1, owners, start_rows, 0)
+    early = owners - per if slots > 2 * chunk else owners
+    lax.fori_loop(1, early, start_rows, 0)
     gates[0] = gate_ref[me]
 
     def send_back(step):
@@ -833,7 +923,7 @@
         back_sum[...] = jnp.zeros_like(back_sum)
 
         def through(step, carry):
-            columns = pl.ds(pl.multiple_of(step * tile, tile), tile)
+            columns = pl.ds(pl.multiple_of(step * 512, 512), 512)
             before = dot(rows[part, :], up[:, columns])
             act_grad = dot(cots[part, :], down[columns, :], 1, 1)
             chance = normal_cdf(before)
@@ -848,7 +938,7 @@
             back_sum[...] += dot(pre_grad, up[:, columns], 1, 1)
             return carry
 
-        lax.fori_loop(0, hidden // tile, through, 0)
+        lax.fori_loop(0, hidden // 512, through, 0)
         back_rows[part, :] = back_sum[...].astype(BF16)
         produced = out_sum[...]
         inner = jnp.sum(produced * cots[part, :].astype(F32), axis=1, keepdims=True)
@@ -872,6 +962,7 @@
         if index == 0:
             home_own.start()
             dot_ref[me] = dots[0]
+            lax.fori_loop(early, owners, start_rows, 0)
     for y_copy in y_copies[-2:]:
         y_copy.wait()
 

time: 433 us -> 422 us (0.975); the launches traced: 431 us -> 413 us
  Pallas kernels: 407 us -> 389 us
    pallas_call x1, Pallas kernels: 176 us -> 163 us  [backward(): pl.pallas_call(functools.partial(backward_kernel, owners, experts, bucket...]
    pallas_call x1, Pallas kernels: 85.8 us -> 80 us  [forward(): pl.pallas_call(functools.partial(forward_kernel, owners, experts, buckets...]
where the time goes in v2:
time: 422 us; the launch traced here: 413 us
  Pallas kernels  389 us (92%)
  local copies, waits for them, and re-layouts  21.1 us (5%)
    pallas_call x1, Pallas kernels, backward(): pl.pallas_call(functools.partial(backward_kernel, owners, experts, bucket...  163 us
    pallas_call x1, Pallas kernels, experts_of(): pl.pallas_call(functools.partial(expert_kernel, owners), out_shape=(shape...  146 us
    pallas_call x1, Pallas kernels, forward(): pl.pallas_call(functools.partial(forward_kernel, owners, experts, buckets...  80 us
    unnamed x24, local copies, waits for them, and re-layouts  15.4 us

profile of v2, /device:TPU:12, one launch (start us, length us, event | category | flops | bytes accessed | tf_op | source)
XLA Modules:
  0.0 413.3 jit_solution(11704463465731088519)
XLA Ops:
  0.6 0.7 broadcast_in_dim.16
  1.3 0.7 broadcast_in_dim.17
  2.0 0.7 pad_maximum_fusion
  2.7 1.0 dynamic_update_slice.6
  3.7 0.8 copy.23
  4.5 0.3 dynamic_update_slice.7.small_part_ref
  4.9 1.3 bitcast_add_fusion.place_ref
  6.2 80.0 %attention_forward.1 = (f32[512,768]{1,0:T(8,128)}, bf16[512,768]{1,0:T(8,128)(2,1)}, bf16[512,2304]{1,0:T(8,128)(2,1)}, bf16[512,768]{1,0:T(8,128)(2,1)}, bf16[...) custom-call(f32[512,768]{1,0:T(8,128)} %x_hbm.1, ...), custom_call_target="tpu_custom_call" | custom-call | flops 12000000000 | bytes 20000000 | tf_op jit(solution)/shard_map/attention_forward/pallas_call | solution.py:722
  86.1 145.8 %experts.1 = (bf16[2048,768]{1,0:T(8,128)(2,1)}, bf16[2048,768]{1,0:T(8,128)(2,1)}, f32[16,1,128]{2,1,0:T(1,128)}, f32[768,1536]{1,0:T(8,128)}, f32[1536,768]{1,0:T(8,128)}) custom-call(bf16[2048,768]{1,0:T(8,128)(2,1)} %get-tuple-element.38.x_ref, f32[16,1,128]{2,1,0:T(1,128)} %get-tuple-element.39.gate_ref, bf16[2048,768]{1,0:T(8,128)(2,1)} %get-tuple-element.40.cot_ref, ...), custom_call_target="tpu_custom_call" | custom-call | flops 57999998976 | bytes 40000000 | tf_op jit(solution)/shard_map/experts/pallas_call | solution.py:1065
  231.9 163.3 %attention_backward.1 = (f32[512,768]{1,0:T(8,128)}, f32[512,768]{1,0:T(8,128)}, f32[384,2304]{1,0:T(8,128)}, f32[384,768]{1,0:T(8,128)}, f32[32,768]{1,0:T(8,128)}) custom-call(f32[512,768]{1,0:T(8,128)} %x_hbm.1, f32[512,768]{1,0:T(8,128)} %cot_hbm.1, f32[512,768]{1,0:T(8,128)} %get-tuple-element.32.hidden_hbm, ...), custom_call_target="tpu_custom_call" | custom-call | flops 24999999488 | bytes 30000000 | tf_op jit(solution)/shard_map/attention_backward/pallas_call | solution.py:780
  395.2 1.0 slice.12
  396.2 0.6 dynamic-slice_bitcast_fusion
  396.8 0.7 dynamic-slice_reduce_fusion
  397.5 0.8 dynamic-slice_bitcast_fusion.1
  398.3 0.7 copy.24
  398.9 2.8 copy.33
  401.7 1.1 copy.34
  402.9 1.8 copy.35
  404.7 1.4 copy-done.2
  406.1 1.0 copy.36
  407.1 2.4 copy.37
  409.5 0.8 slice-done
  410.4 0.3 slice-done.1
  410.7 2.2 copy.38
  (16 shorter events, 0.0 us)
Async XLA Ops:
  4.8 1.3 copy-start.3
  395.2 6.6 %copy-start.1 = (f32[512,768]{1,0:T(8,128)S(1)}, f32[512,768]{1,0:T(8,128)}, u32[]{:S(2)}) copy-start(f32[512,768]{1,0:T(8,128)} %get-tuple-element.77) | copy-start | bytes 4718596
  398.9 4.0 copy-start
  401.7 5.4 %slice-start.2 = ((s8[4718592]{0:T(1024)(128)(4,1)}), s8[4194304]{0:T(1024)(128)(4,1)S(1)}, s32[]{:S(2)}) async-start(s8[4718592]{0:T(1024)(128)(4,1)} %bitcast.17), calls=%async_computation.2 | async-start | bytes 8388608
  402.9 3.2 copy-start.2
  402.9 4.2 %slice-start.3 = ((s8[4718592]{0:T(1024)(128)(4,1)}), s8[524288]{0:T(1024)(128)(4,1)S(1)}, s32[]{:S(2)}) async-start(s8[4718592]{0:T(1024)(128)(4,1)} %bitcast.17), calls=%async_computation.3 | async-start | bytes 1048576
  406.1 4.3 %slice-start = ((s8[4718592]{0:T(1024)(128)(4,1)}), s8[4194304]{0:T(1024)(128)(4,1)S(1)}, s32[]{:S(2)}) async-start(s8[4718592]{0:T(1024)(128)(4,1)} %bitcast.14), calls=%async_computation | async-start | bytes 8388608
  407.1 3.5 slice-start.1

commit v3 on v2

--- a/solution.py
+++ b/solution.py
@@ -896,22 +896,26 @@
         )
 
     home_own = pltpu.make_async_copy(back_rows.at[block(0)], home_ref.at[block(me)], own_sem.at[1])
-    y_copies = []
-    for index in range(slots // chunk):
+    chunks = slots // chunk
+
+    def y_copy(index):
+        slot = lax.rem(index, 2)
+        part = pl.ds(pl.multiple_of(index * chunk, chunk), chunk)
+        return pltpu.make_async_copy(y_rows.at[slot], y_ref.at[part], y_sem.at[slot])
+
+    def arrive(step, carry):
+        for copy in send_rows(step):
+            copy.wait_recv()
+        return carry
+
+    def start_back(step, carry):
+        for copy in send_back(step):
+            copy.start()
+        return carry
+
+    def process(index):
         first = index * per
-        part = slice(index * chunk, (index + 1) * chunk)
-        if index == 0:
-            own_rows.wait()
-            load_cots.wait()
-            load_up.wait()
-            load_down.wait()
-
-        def arrive(step, carry):
-            for copy in send_rows(step):
-                copy.wait_recv()
-            return carry
-
-        lax.fori_loop(max(first, 1), first + per, arrive, 0)
+        part = pl.ds(pl.multiple_of(index * chunk, chunk), chunk)
         column = jnp.concatenate(
             [
                 jnp.transpose(jnp.broadcast_to(gates[first + b], (BLOCK, capacity)))[:, 0:1]
@@ -921,9 +925,10 @@
         )
         out_sum[...] = jnp.zeros_like(out_sum)
         back_sum[...] = jnp.zeros_like(back_sum)
+        stretch = min(hidden, 512)
 
         def through(step, carry):
-            columns = pl.ds(pl.multiple_of(step * 512, 512), 512)
+            columns = pl.ds(pl.multiple_of(step * stretch, stretch), stretch)
             before = dot(rows[part, :], up[:, columns])
             act_grad = dot(cots[part, :], down[columns, :], 1, 1)
             chance = normal_cdf(before)
@@ -938,7 +943,7 @@
             back_sum[...] += dot(pre_grad, up[:, columns], 1, 1)
             return carry
 
-        lax.fori_loop(0, hidden // 512, through, 0)
+        lax.fori_loop(0, hidden // stretch, through, 0)
         back_rows[part, :] = back_sum[...].astype(BF16)
         produced = out_sum[...]
         inner = jnp.sum(produced * cots[part, :].astype(F32), axis=1, keepdims=True)
@@ -946,25 +951,42 @@
         for b in range(per):
             turned = jnp.transpose(spread[b * capacity : (b + 1) * capacity, :])
             dots[first + b] = turned[0:1, :]
-        if index >= 2:
-            y_copies[index - 2].wait()
-        y_rows[index % 2] = (produced * column).astype(BF16)
-        y_copy = pltpu.make_async_copy(y_rows.at[index % 2], y_ref.at[part], y_sem.at[index % 2])
-        y_copy.start()
-        y_copies.append(y_copy)
-
-        def start_back(step, carry):
-            for copy in send_back(step):
-                copy.start()
-            return carry
-
-        lax.fori_loop(max(first, 1), first + per, start_back, 0)
-        if index == 0:
-            home_own.start()
-            dot_ref[me] = dots[0]
-            lax.fori_loop(early, owners, start_rows, 0)
-    for y_copy in y_copies[-2:]:
-        y_copy.wait()
+        return (produced * column).astype(BF16)
+
+    own_rows.wait()
+    load_cots.wait()
+    load_up.wait()
+    load_down.wait()
+    lax.fori_loop(1, per, arrive, 0)
+    y_rows[0] = process(jnp.int32(0))
+    y_copy(jnp.int32(0)).start()
+    lax.fori_loop(1, per, start_back, 0)
+    home_own.start()
+    dot_ref[me] = dots[0]
+    lax.fori_loop(early, owners, start_rows, 0)
+
+    def later(index, carry):
+        def arrive_in(b, carry):
+            return arrive(index * per + b, carry)
+
+        def start_in(b, carry):
+            return start_back(index * per + b, carry)
+
+        lax.fori_loop(0, per, arrive_in, 0)
+        result = process(index)
+
+        @pl.when(index >= 2)
+        def _():
+            y_copy(index - 2).wait()
+
+        y_rows[lax.rem(index, 2)] = result
+        y_copy(index).start()
+        lax.fori_loop(0, per, start_in, 0)
+        return carry
+
+    lax.fori_loop(1, chunks, later, 0)
+    for index in range(max(chunks - 2, 0), chunks):
+        y_copy(jnp.int32(index)).wait()
 
     half = hidden // 2
     count = half // tile

time: 422 us -> 414 us (0.981); the launches traced: 413 us -> 413 us
  no operation moved by 1% of the time
where the time goes in v3:
time: 414 us; the launch traced here: 413 us
  Pallas kernels  389 us (94%)
  local copies, waits for them, and re-layouts  21.1 us (5%)
    pallas_call x1, Pallas kernels, backward(): pl.pallas_call(functools.partial(backward_kernel, owners, experts, bucket...  164 us
    pallas_call x1, Pallas kernels, experts_of(): pl.pallas_call(functools.partial(expert_kernel, owners), out_shape=(shape...  146 us
    pallas_call x1, Pallas kernels, forward(): pl.pallas_call(functools.partial(forward_kernel, owners, experts, buckets...  80 us
    unnamed x24, local copies, waits for them, and re-layouts  15.4 us

profile of v3, /device:TPU:12, one launch (start us, length us, event | category | flops | bytes accessed | tf_op | source)
XLA Modules:
  0.0 413.2 jit_solution(6932346650086148040)
XLA Ops:
  0.6 0.7 broadcast_in_dim.16
  1.3 0.7 broadcast_in_dim.17
  2.0 0.7 pad_maximum_fusion
  2.7 1.0 dynamic_update_slice.6
  3.7 0.8 copy.23
  4.5 0.3 dynamic_update_slice.7.small_part_ref
  4.9 1.3 bitcast_add_fusion.place_ref
  6.2 80.0 %attention_forward.1 = (f32[512,768]{1,0:T(8,128)}, bf16[512,768]{1,0:T(8,128)(2,1)}, bf16[512,2304]{1,0:T(8,128)(2,1)}, bf16[512,768]{1,0:T(8,128)(2,1)}, bf16[...) custom-call(f32[512,768]{1,0:T(8,128)} %x_hbm.1, ...), custom_call_target="tpu_custom_call" | custom-call | flops 12000000000 | bytes 20000000 | tf_op jit(solution)/shard_map/attention_forward/pallas_call | solution.py:722
  86.2 145.8 %experts.1 = (bf16[2048,768]{1,0:T(8,128)(2,1)}, bf16[2048,768]{1,0:T(8,128)(2,1)}, f32[16,1,128]{2,1,0:T(1,128)}, f32[768,1536]{1,0:T(8,128)}, f32[1536,768]{1,0:T(8,128)}) custom-call(bf16[2048,768]{1,0:T(8,128)(2,1)} %get-tuple-element.38.x_ref, f32[16,1,128]{2,1,0:T(1,128)} %get-tuple-element.39.gate_ref, bf16[2048,768]{1,0:T(8,128)(2,1)} %get-tuple-element.40.cot_ref, ...), custom_call_target="tpu_custom_call" | custom-call | flops 57999998976 | bytes 40000000 | tf_op jit(solution)/shard_map/experts/pallas_call | solution.py:1087
  232.0 163.5 %attention_backward.1 = (f32[512,768]{1,0:T(8,128)}, f32[512,768]{1,0:T(8,128)}, f32[384,2304]{1,0:T(8,128)}, f32[384,768]{1,0:T(8,128)}, f32[32,768]{1,0:T(8,128)}) custom-call(f32[512,768]{1,0:T(8,128)} %x_hbm.1, f32[512,768]{1,0:T(8,128)} %cot_hbm.1, f32[512,768]{1,0:T(8,128)} %get-tuple-element.32.hidden_hbm, ...), custom_call_target="tpu_custom_call" | custom-call | flops 24999999488 | bytes 30000000 | tf_op jit(solution)/shard_map/attention_backward/pallas_call | solution.py:780
  395.5 1.0 slice.12
  396.5 0.6 dynamic-slice_bitcast_fusion
  397.1 0.7 dynamic-slice_reduce_fusion
  397.8 0.8 dynamic-slice_bitcast_fusion.1
  398.6 0.7 copy.24
  399.2 2.8 copy.33
  402.0 1.1 copy.34
  403.2 1.8 copy.35
  405.0 1.4 copy-done.2
  406.4 1.0 copy.36
  407.5 2.4 copy.37
  409.9 0.8 slice-done
  410.7 0.3 slice-done.1
  411.0 2.2 copy.38
  (16 shorter events, 0.0 us)
Async XLA Ops:
  4.8 1.3 copy-start.3
  395.5 6.6 %copy-start.1 = (f32[512,768]{1,0:T(8,128)S(1)}, f32[512,768]{1,0:T(8,128)}, u32[]{:S(2)}) copy-start(f32[512,768]{1,0:T(8,128)} %get-tuple-element.77) | copy-start | bytes 4718596
  399.2 4.0 copy-start
  402.0 5.4 %slice-start.2 = ((s8[4718592]{0:T(1024)(128)(4,1)}), s8[4194304]{0:T(1024)(128)(4,1)S(1)}, s32[]{:S(2)}) async-start(s8[4718592]{0:T(1024)(128)(4,1)} %bitcast.17), calls=%async_computation.2 | async-start | bytes 8388608
  403.2 3.2 copy-start.2
  403.2 4.2 %slice-start.3 = ((s8[4718592]{0:T(1024)(128)(4,1)}), s8[524288]{0:T(1024)(128)(4,1)S(1)}, s32[]{:S(2)}) async-start(s8[4718592]{0:T(1024)(128)(4,1)} %bitcast.17), calls=%async_computation.3 | async-start | bytes 1048576
  406.4 4.3 %slice-start = ((s8[4718592]{0:T(1024)(128)(4,1)}), s8[4194304]{0:T(1024)(128)(4,1)S(1)}, s32[]{:S(2)}) async-start(s8[4718592]{0:T(1024)(128)(4,1)} %bitcast.14), calls=%async_computation | async-start | bytes 8388608
  407.4 3.5 slice-start.1

commit v4 on v3

--- a/solution.py
+++ b/solution.py
@@ -877,8 +877,7 @@
             copy.start()
         return carry
 
-    early = owners - per if slots > 2 * chunk else owners
-    lax.fori_loop(1, early, start_rows, 0)
+    lax.fori_loop(1, owners, start_rows, 0)
     gates[0] = gate_ref[me]
 
     def send_back(step):
@@ -925,7 +924,7 @@
         )
         out_sum[...] = jnp.zeros_like(out_sum)
         back_sum[...] = jnp.zeros_like(back_sum)
-        stretch = min(hidden, 512)
+        stretch = hidden // 4
 
         def through(step, carry):
             columns = pl.ds(pl.multiple_of(step * stretch, stretch), stretch)
@@ -963,7 +962,6 @@
     lax.fori_loop(1, per, start_back, 0)
     home_own.start()
     dot_ref[me] = dots[0]
-    lax.fori_loop(early, owners, start_rows, 0)
 
     def later(index, carry):
         def arrive_in(b, carry):

time: 414 us -> 413 us (level)
  no operation moved by 1% of the time
where the time goes in v4:
time: 413 us; the launch traced here: 412 us
  Pallas kernels  388 us (94%)
  local copies, waits for them, and re-layouts  21.1 us (5%)
    pallas_call x1, Pallas kernels, backward(): pl.pallas_call(functools.partial(backward_kernel, owners, experts, bucket...  163 us
    pallas_call x1, Pallas kernels, experts_of(): pl.pallas_call(functools.partial(expert_kernel, owners), out_shape=(shape...  145 us
    pallas_call x1, Pallas kernels, forward(): pl.pallas_call(functools.partial(forward_kernel, owners, experts, buckets...  80 us
    unnamed x24, local copies, waits for them, and re-layouts  15.4 us

profile of v4, /device:TPU:12, one launch (start us, length us, event | category | flops | bytes accessed | tf_op | source)
XLA Modules:
  0.0 412.2 jit_solution(3472816422531320744)
XLA Ops:
  0.6 0.7 broadcast_in_dim.16
  1.3 0.7 broadcast_in_dim.17
  2.0 0.7 pad_maximum_fusion
  2.7 1.0 dynamic_update_slice.6
  3.7 0.8 copy.23
  4.5 0.3 dynamic_update_slice.7.small_part_ref
  4.9 1.3 bitcast_add_fusion.place_ref
  6.2 80.0 %attention_forward.1 = (f32[512,768]{1,0:T(8,128)}, bf16[512,768]{1,0:T(8,128)(2,1)}, bf16[512,2304]{1,0:T(8,128)(2,1)}, bf16[512,768]{1,0:T(8,128)(2,1)}, bf16[...) custom-call(f32[512,768]{1,0:T(8,128)} %x_hbm.1, ...), custom_call_target="tpu_custom_call" | custom-call | flops 12000000000 | bytes 20000000 | tf_op jit(solution)/shard_map/attention_forward/pallas_call | solution.py:722
  86.2 145.2 %experts.1 = (bf16[2048,768]{1,0:T(8,128)(2,1)}, bf16[2048,768]{1,0:T(8,128)(2,1)}, f32[16,1,128]{2,1,0:T(1,128)}, f32[768,1536]{1,0:T(8,128)}, f32[1536,768]{1,0:T(8,128)}) custom-call(bf16[2048,768]{1,0:T(8,128)(2,1)} %get-tuple-element.38.x_ref, f32[16,1,128]{2,1,0:T(1,128)} %get-tuple-element.39.gate_ref, bf16[2048,768]{1,0:T(8,128)(2,1)} %get-tuple-element.40.cot_ref, ...), custom_call_target="tpu_custom_call" | custom-call | flops 57999998976 | bytes 40000000 | tf_op jit(solution)/shard_map/experts/pallas_call | solution.py:1085
  231.3 163.2 %attention_backward.1 = (f32[512,768]{1,0:T(8,128)}, f32[512,768]{1,0:T(8,128)}, f32[384,2304]{1,0:T(8,128)}, f32[384,768]{1,0:T(8,128)}, f32[32,768]{1,0:T(8,128)}) custom-call(f32[512,768]{1,0:T(8,128)} %x_hbm.1, f32[512,768]{1,0:T(8,128)} %cot_hbm.1, f32[512,768]{1,0:T(8,128)} %get-tuple-element.32.hidden_hbm, ...), custom_call_target="tpu_custom_call" | custom-call | flops 24999999488 | bytes 30000000 | tf_op jit(solution)/shard_map/attention_backward/pallas_call | solution.py:780
  394.5 1.0 slice.12
  395.5 0.6 dynamic-slice_bitcast_fusion
  396.1 0.7 dynamic-slice_reduce_fusion
  396.8 0.8 dynamic-slice_bitcast_fusion.1
  397.6 0.7 copy.24
  398.2 2.8 copy.33
  401.1 1.1 copy.34
  402.2 1.8 copy.35
  404.0 1.4 copy-done.2
  405.4 1.0 copy.36
  406.5 2.4 copy.37
  408.9 0.8 slice-done
  409.7 0.3 slice-done.1
  410.0 2.2 copy.38
  (16 shorter events, 0.0 us)
Async XLA Ops:
  4.8 1.3 copy-start.3
  394.5 6.6 %copy-start.1 = (f32[512,768]{1,0:T(8,128)S(1)}, f32[512,768]{1,0:T(8,128)}, u32[]{:S(2)}) copy-start(f32[512,768]{1,0:T(8,128)} %get-tuple-element.77) | copy-start | bytes 4718596
  398.2 4.0 copy-start
  401.1 5.4 %slice-start.2 = ((s8[4718592]{0:T(1024)(128)(4,1)}), s8[4194304]{0:T(1024)(128)(4,1)S(1)}, s32[]{:S(2)}) async-start(s8[4718592]{0:T(1024)(128)(4,1)} %bitcast.17), calls=%async_computation.2 | async-start | bytes 8388608
  402.2 3.2 copy-start.2
  402.2 4.2 %slice-start.3 = ((s8[4718592]{0:T(1024)(128)(4,1)}), s8[524288]{0:T(1024)(128)(4,1)S(1)}, s32[]{:S(2)}) async-start(s8[4718592]{0:T(1024)(128)(4,1)} %bitcast.17), calls=%async_computation.3 | async-start | bytes 1048576
  405.4 4.3 %slice-start = ((s8[4718592]{0:T(1024)(128)(4,1)}), s8[4194304]{0:T(1024)(128)(4,1)S(1)}, s32[]{:S(2)}) async-start(s8[4718592]{0:T(1024)(128)(4,1)} %bitcast.14), calls=%async_computation | async-start | bytes 8388608
  406.5 3.5 slice-start.1
